TPU v7x, 512 devices: a whole 4x4x16 slice. The times are simulated.
512 devices in a mesh: cross: 16 (over y_hi, x, core), along: 32 (over z, y_lo).
Axes of the slice: x: 4, y: 4 (y_hi: 2, y_lo: 2; y = y_hi * 2 + y_lo), z: 16, core: 2. Of those that a mesh axis runs over, the one named last changes fastest.
Arguments:
- surface: float32 [4096, 8192], P('cross', 'along'), may hold values from -6 to 6
- flux_cross: float32 [4096, 8192], P('cross', 'along'), may hold values from -6 to 6
- flux_along: float32 [4096, 8192], P('cross', 'along'), may hold values from -6 to 6
- celerity_sq: float32 [4096, 8192], P('cross', 'along'), may hold values from 0.05 to 1
- wet_mask: int32 [4096, 8192], P('cross', 'along'), may hold values from 0 to 1, as said below
- range_test: float32 [8192, 128], P('along'), may hold values from -0.0625 to 0.0625
- corange_test: float32 [128, 4096], P(None, 'cross'), may hold values from -0.09375 to 0.09375
- core_left: float32 [256, 4096], P(None, 'cross'), may hold values from -0.09375 to 0.09375
- core_right: float32 [8192, 256], P('along'), may hold values from -0.0625 to 0.0625
Outputs:
- surface_next: float32 [4096, 8192], P('cross', 'along')
- flux_cross_next: float32 [4096, 8192], P('cross', 'along')
- flux_along_next: float32 [4096, 8192], P('cross', 'along')
- range_sketch: float32 [4096, 128], P('cross')
- corange_sketch: float32 [128, 8192], P(None, 'along')
- core_sketch: float32 [256, 256], replicated
Inputs may be any that keep to these rules, and one draw needn't show every extreme that they name: `wet_mask`: 1 marks a wet cell, 0 a dry one.
All inputs are finite; a program needn't handle non-finite values.
Results may differ from a plain program's by a relative error of at most 0.000073.
Values sent between devices are 32-bit elements; how exact they have to be, the bound alone decides.
A program may use at most 64 MiB of HBM per device.

v0:
```python
import jax
import jax.numpy as jnp
from jax import lax
from jax.sharding import PartitionSpec as P


def with_halo(block, sides, width):
    for axis, dim in sides:
        count = lax.axis_size(axis)
        forward = [(i, i + 1) for i in range(count - 1)]
        backward = [(target, source) for source, target in forward]
        low = lax.ppermute(
            lax.slice_in_dim(block, block.shape[dim] - width, None, axis=dim), axis, forward
        )
        high = lax.ppermute(lax.slice_in_dim(block, 0, width, axis=dim), axis, backward)
        block = jnp.concatenate([low, block, high], axis=dim)
    return block


def cut_along(array, dim, count):
    dims = array.shape
    pieces = array.reshape(*dims[:dim], count, dims[dim] // count, *dims[dim + 1 :])
    return jnp.moveaxis(pieces, dim, 0)


def summed_on_arrival(array, axis, dim):
    pieces = cut_along(array, dim, lax.axis_size(axis))
    arrived = lax.all_to_all(pieces, axis, split_axis=0, concat_axis=0, tiled=True)
    return arrived.sum(axis=0)


def padded_to(lines, count):
    spare = -len(lines) % count
    return jnp.pad(lines, [(0, spare)] + [(0, 0)] * (lines.ndim - 1))


def copy_for_each(array, axis):
    copies = jnp.broadcast_to(array, (lax.axis_size(axis), *array.shape))
    return lax.all_to_all(copies, axis, split_axis=0, concat_axis=0, tiled=True)


def laid_out(pieces, dim):
    dims = list(pieces.shape[1:])
    dims[dim] *= pieces.shape[0]
    return jnp.moveaxis(pieces, 0, dim).reshape(dims)


def gathered_copies(array, axis, dim):
    pieces = copy_for_each(array, axis)
    return laid_out(pieces, dim)


def total_of(array, axes):
    own = summed_on_arrival(padded_to(array, lax.axis_size(axes)), axes, 0)
    whole = gathered_copies(own, axes, 0)
    return whole[: len(array)].reshape(array.shape)


def packed_total(arrays, axis):
    ravelled, at, gathered = (jnp.concatenate([a.reshape(-1) for a in arrays]), 0, [])
    subtotal = total_of(ravelled, axis)
    for a in arrays:
        gathered.append(subtotal[at : at + a.size].reshape(a.shape))
        at += a.size
    return tuple(gathered)


def derive(padded, axis):
    count = padded.shape[axis] - 4

    def part(start):
        return lax.slice_in_dim(padded, start, start + count, axis=axis)

    return (8.0 * (part(3) - part(1)) - (part(4) - part(0))) / 12.0


def inner_cycle(field):
    return field[2:-2, 2:-2]


def shrinking_tendency(elev, flux_x, flux_y, wet, celerity_sq):
    masked_x = wet * flux_x
    masked_y = wet * flux_y
    inner_wet = inner_cycle(wet)
    inner_cel = inner_cycle(celerity_sq)
    d_elev = -0.25 * inner_wet * (derive(masked_x, 0)[:, 2:-2] + derive(masked_y, 1)[2:-2, :])
    friction = 0.02 / inner_cel
    d_flux_x = -inner_wet * (
        0.25 * inner_cel * derive(elev, 0)[:, 2:-2] + friction * inner_cycle(flux_x)
    )
    d_flux_y = -inner_wet * (
        0.25 * inner_cel * derive(elev, 1)[2:-2, :] + friction * inner_cycle(flux_y)
    )
    return (d_elev, d_flux_x, d_flux_y)


def body(
    surface,
    flux_cross,
    flux_along,
    celerity_sq,
    wet_mask,
    range_test,
    corange_test,
    core_left,
    core_right,
):
    wet = wet_mask.astype(jnp.float32)
    state = jnp.stack([surface, flux_cross, flux_along, celerity_sq, wet])
    padded = with_halo(state, (("cross", 1), ("along", 2)), 4)
    elev_pad = padded[0]
    fx_pad = padded[1]
    fy_pad = padded[2]
    cel_pad = jnp.where(padded[3] > 0.0, padded[3], 1.0)
    wet_pad = padded[4]
    k1e, k1p, k1q = shrinking_tendency(elev_pad, fx_pad, fy_pad, wet_pad, cel_pad)
    mid_wet = inner_cycle(wet_pad)
    mid_cel = inner_cycle(cel_pad)
    k2e, k2p, k2q = shrinking_tendency(
        inner_cycle(elev_pad) + k1e,
        inner_cycle(fx_pad) + k1p,
        inner_cycle(fy_pad) + k1q,
        mid_wet,
        mid_cel,
    )
    k1e = inner_cycle(k1e)
    k1p = inner_cycle(k1p)
    k1q = inner_cycle(k1q)
    surface_next = surface + 0.5 * (k1e + k2e)
    flux_cross_next = flux_cross + 0.5 * (k1p + k2p)
    flux_along_next = flux_along + 0.5 * (k1q + k2q)
    high = lax.Precision.HIGHEST
    range_part = jnp.dot(
        surface_next, range_test, precision=high, preferred_element_type=jnp.float32
    )
    corange_part = jnp.dot(
        corange_test, surface_next, precision=high, preferred_element_type=jnp.float32
    )
    right_part = jnp.dot(
        surface_next, core_right, precision=high, preferred_element_type=jnp.float32
    )
    range_sketch, right_rows = packed_total((range_part, right_part), "along")
    core_part = jnp.dot(core_left, right_rows, precision=high, preferred_element_type=jnp.float32)
    corange_sketch, core_sketch = packed_total((corange_part, core_part), "cross")
    return (
        surface_next,
        flux_cross_next,
        flux_along_next,
        range_sketch,
        corange_sketch,
        core_sketch,
    )


def solution(mesh):
    return jax.shard_map(
        body,
        mesh=mesh,
        in_specs=(
            P("cross", "along"),
            P("cross", "along"),
            P("cross", "along"),
            P("cross", "along"),
            P("cross", "along"),
            P("along", None),
            P(None, "cross"),
            P(None, "cross"),
            P("along", None),
        ),
        out_specs=(
            P("cross", "along"),
            P("cross", "along"),
            P("cross", "along"),
            P("cross", None),
            P(None, "along"),
            P(),
        ),
        check_vma=False,
    )
```

profile of v0, /device:TPU:1, one launch (start us, length us, event | category | flops | bytes accessed | tf_op | source)
XLA Modules:
  0.0 145.8 jit_solution(9457546303489990771)
XLA Ops:
  0.7 1.0 bitcast_dynamic-update-slice_fusion.4
  1.7 1.0 bitcast_dynamic-update-slice_fusion.3
  2.7 1.0 bitcast_dynamic-update-slice_fusion.2
  3.8 4.5 %collective-permute-start = (f32[5,4,256]{2,1,0:T(4,128)S(1)}, f32[5,4,256]{2,1,0:T(4,128)S(1)}, u32[]{:S(2)}, u32[]{:S(2)}) collective-permute-start(f32[5,4,256]{2,1,0:T(4,128)S(1)} %get-tuple-element.29), channel_id=1, source_target_pairs={{0,32},{32,64},{64,96},{96,128},{128,160},{160,192},{192,224},{224... | collective-permute-start | bytes 61448 | tf_op jit(solution)/shard_map/ppermute | solution.py:12
  8.3 5.5 %collective-permute-start.1 = (f32[5,4,256]{2,1,0:T(4,128)S(1)}, f32[5,4,256]{2,1,0:T(4,128)S(1)}, u32[]{:S(2)}, u32[]{:S(2)}) collective-permute-start(f32[5,4,256]{2,1,0:T(4,128)S(1)} %get-tuple-element.30), channel_id=1, source_target_pairs={{32,0},{64,32},{96,64},{128,96},{160,128},{192,160},{224,192},{256... | collective-permute-start | bytes 61448 | tf_op jit(solution)/shard_map/ppermute | solution.py:15
  13.8 0.8 collective-permute-done.1
  15.3 1.9 %collective-permute-start.2 = (f32[5,264,4]{1,2,0:T(4,128)S(1)}, f32[5,264,4]{1,2,0:T(4,128)S(1)}, u32[]{:S(2)}, u32[]{:S(2)}) collective-permute-start(f32[5,264,4]{1,2,0:T(4,128)S(1)} %copy.42), channel_id=1, source_target_pairs={{0,1},{1,2},{2,3},{3,4},{4,5},{5,6},{6,7},{7,8},{8,9},{9,10},{10,1... | collective-permute-start | bytes 63368 | tf_op jit(solution)/shard_map/ppermute | solution.py:12
  17.6 1.3 collective-permute-start.3
  19.2 3.7 %collective-permute-done.3 = f32[5,264,4]{1,2,0:T(4,128)S(1)} collective-permute-done((f32[5,264,4]{1,2,0:T(4,128)S(1)}, f32[5,264,4]{1,2,0:T(4,128)S(1)}, u32[]{:S(2)}, u32[]{:S(2)}) %collective-permute-start.3) | collective-permute-done | bytes 21152 | tf_op jit(solution)/shard_map/ppermute | solution.py:15
  23.1 0.8 pad_maximum_fusion
  25.2 1.6 %slice_multiply_fusion.3 = (f32[260,260]{1,0:T(8,128)S(1)}, f32[260,260]{1,0:T(8,128)S(1)}, f32[260,260]{1,0:T(8,128)S(1)}, f32[260,260]{1,0:T(8,128)S(1)}, f32[260,260]{1,0:T(8,128)}, /*index=5*/f32[260,260]{1,0:T(8,128)}) fusion(f32[264,264]{1,0:T(8,128)S(1)} %get-tuple-element.26, f32[264,264]{1,0:T(8,128)S(1)} %get-tuple-element.23, ...), kind=kLoop, calls=%fused_computation.49 | loop fusion | flops 1352000 | bytes 4056000 | tf_op jit(solution)/shard_map/mul | solution.py:82
  27.2 0.8 slice_add_fusion
  30.2 44.3 %all_to_all.30 = f32[32,1,3072]{2,1,0:T(1,128)S(1)} all-to-all(f32[32,1,3072]{2,1,0:T(1,128)S(1)} %bitcast.56), channel_id=1, replica_groups=mesh['cross'=16,'along'=32] {'along'}, dimensions={0} | all-to-all | bytes 786432 | tf_op jit(solution)/shard_map/all_to_all | solution.py:28
  74.7 1.0 broadcast_in_dim.11
  75.6 3.9 %all-to-all-start.1 = ((f32[32,1,3072]{2,1,0:T(1,128)}), f32[32,1,3072]{2,1,0:T(1,128)S(1)}, u32[]{:S(2)}, u32[]{:S(2)}) async-start(f32[32,1,3072]{2,1,0:T(1,128)} %broadcast_in_dim.11), calls=%async_computation.1 | async-start | bytes 786432 | tf_op jit(solution)/shard_map/all_to_all | solution.py:39
  80.2 0.7 copy.53
  81.0 24.8 %all-to-all-done.1 = f32[32,1,3072]{2,1,0:T(1,128)S(1)} async-done(((f32[32,1,3072]{2,1,0:T(1,128)}), f32[32,1,3072]{2,1,0:T(1,128)S(1)}, u32[]{:S(2)}, u32[]{:S(2)}) %all-to-all-start.1) | async-done | bytes 393248 | tf_op jit(solution)/shard_map/all_to_all | solution.py:39
  105.8 0.9 reduce.2
  106.8 1.6 %convolution_bitcast_fusion.1 = f32[256,256]{0,1:T(8,128)S(1)} fusion(f32[256,256]{1,0:T(8,128)} %param.16, f32[384,256]{1,0:T(8,128)S(1)} %slice.283), kind=kOutput, calls=%fused_computation.4 | convolution fusion | flops 201326592 | bytes 786432 | tf_op jit(solution)/shard_map/dot_general | solution.py:143
  108.7 1.7 %pad_maximum_fusion.3 = f32[98304]{0:T(1024)} fusion(f32[65536]{0:T(1024)S(1)} %bitcast.58, f32[32768]{0:T(1024)} %bitcast.61), kind=kLoop, calls=%fused_computation.43 | loop fusion | flops 98304 | bytes 786432 | tf_op jit(solution)/shard_map/concatenate | solution.py:60
  110.3 8.0 %all-to-all-start.2 = ((f32[16,1,6144]{2,1,0:T(1,128)}), f32[16,1,6144]{2,1,0:T(1,128)S(1)}, u32[]{:S(2)}, u32[]{:S(2)}) async-start(f32[16,1,6144]{2,1,0:T(1,128)} %bitcast.16), calls=%async_computation.2 | async-start | bytes 786432 | tf_op jit(solution)/shard_map/all_to_all | solution.py:28
  118.3 1.1 fusion.58
  119.4 8.6 %all-to-all-done.2 = f32[16,1,6144]{2,1,0:T(1,128)S(1)} async-done(((f32[16,1,6144]{2,1,0:T(1,128)}), f32[16,1,6144]{2,1,0:T(1,128)S(1)}, u32[]{:S(2)}, u32[]{:S(2)}) %all-to-all-start.2) | async-done | bytes 393248 | tf_op jit(solution)/shard_map/all_to_all | solution.py:28
  128.2 1.0 broadcast_in_dim.12
  129.2 4.4 %all-to-all-start.3 = ((f32[16,1,6144]{2,1,0:T(1,128)}), f32[16,1,6144]{2,1,0:T(1,128)S(1)}, u32[]{:S(2)}, u32[]{:S(2)}) async-start(f32[16,1,6144]{2,1,0:T(1,128)} %broadcast_in_dim.12), calls=%async_computation.3 | async-start | bytes 786432 | tf_op jit(solution)/shard_map/all_to_all | solution.py:39
  133.9 0.7 copy-done.2
  135.1 2.6 %fusion.25 = (f32[256,256]{1,0:T(8,128)}, f32[256,256]{1,0:T(8,128)}) fusion(f32[256,256]{1,0:T(8,128)} %param.11, f32[260,260]{1,0:T(8,128)S(1)} %copy-done.2, f32[260,256]{1,0:T(8,128)S(1)} %get-tuple-element.37, f32[260,256]{1,0:T(8,128)S(1)} %get-tuple-element.38, f32[260,256]{1,0:T(8,128)S(1)} %get-tuple-element.39, ...), kind=kLoop, calls=%fused_computation.56 | loop fusion | flops 1769472 | bytes 4718592 | tf_op jit(solution)/shard_map/add | solution.py:131
  137.7 0.7 slice.370
  138.4 5.0 %all-to-all-done.3 = f32[16,1,6144]{2,1,0:T(1,128)S(1)} async-done(((f32[16,1,6144]{2,1,0:T(1,128)}), f32[16,1,6144]{2,1,0:T(1,128)S(1)}, u32[]{:S(2)}, u32[]{:S(2)}) %all-to-all-start.3) | async-done | bytes 393248 | tf_op jit(solution)/shard_map/all_to_all | solution.py:39
  143.4 0.9 reduce.3
  144.4 0.7 slice.373
  145.1 0.7 slice.372
  (56 shorter events, 7.7 us)
Async XLA Ops:
  0.6 28.1 %copy-start = (f32[256,256]{1,0:T(8,128)S(1)}, f32[256,256]{1,0:T(8,128)}, u32[]{:S(2)}) copy-start(f32[256,256]{1,0:T(8,128)} %param.17) | copy-start | bytes 786436
  0.6 3.0 %copy-start.8 = (f32[256,256]{1,0:T(8,128)S(1)}, f32[256,256]{1,0:T(8,128)}, u32[]{:S(2)}) copy-start(f32[256,256]{1,0:T(8,128)} %param.12) | copy-start | bytes 786436
  0.7 3.0 %copy-start.9 = (s32[256,256]{1,0:T(8,128)S(1)}, s32[256,256]{1,0:T(8,128)}, u32[]{:S(2)}) copy-start(s32[256,256]{1,0:T(8,128)} %param.13) | copy-start | bytes 786436
  3.8 10.1 %collective-permute-start = (f32[5,4,256]{2,1,0:T(4,128)S(1)}, f32[5,4,256]{2,1,0:T(4,128)S(1)}, u32[]{:S(2)}, u32[]{:S(2)}) collective-permute-start(f32[5,4,256]{2,1,0:T(4,128)S(1)} %get-tuple-element.29), channel_id=1, source_target_pairs={{0,32},{32,64},{64,96},{96,128},{128,160},{160,192},{192,224},{224... | collective-permute-start | bytes 61448 | tf_op jit(solution)/shard_map/ppermute | solution.py:12
  8.3 6.4 %collective-permute-start.1 = (f32[5,4,256]{2,1,0:T(4,128)S(1)}, f32[5,4,256]{2,1,0:T(4,128)S(1)}, u32[]{:S(2)}, u32[]{:S(2)}) collective-permute-start(f32[5,4,256]{2,1,0:T(4,128)S(1)} %get-tuple-element.30), channel_id=1, source_target_pairs={{32,0},{64,32},{96,64},{128,96},{160,128},{192,160},{224,192},{256... | collective-permute-start | bytes 61448 | tf_op jit(solution)/shard_map/ppermute | solution.py:15
  15.3 3.6 %collective-permute-start.2 = (f32[5,264,4]{1,2,0:T(4,128)S(1)}, f32[5,264,4]{1,2,0:T(4,128)S(1)}, u32[]{:S(2)}, u32[]{:S(2)}) collective-permute-start(f32[5,264,4]{1,2,0:T(4,128)S(1)} %copy.42), channel_id=1, source_target_pairs={{0,1},{1,2},{2,3},{3,4},{4,5},{5,6},{6,7},{7,8},{8,9},{9,10},{10,1... | collective-permute-start | bytes 63368 | tf_op jit(solution)/shard_map/ppermute | solution.py:12
  17.6 5.3 %collective-permute-start.3 = (f32[5,264,4]{1,2,0:T(4,128)S(1)}, f32[5,264,4]{1,2,0:T(4,128)S(1)}, u32[]{:S(2)}, u32[]{:S(2)}) collective-permute-start(f32[5,264,4]{1,2,0:T(4,128)S(1)} %copy.43), channel_id=1, source_target_pairs={{1,0},{2,1},{3,2},{4,3},{5,4},{6,5},{7,6},{8,7},{9,8},{10,9},{11,1... | collective-permute-start | bytes 63368 | tf_op jit(solution)/shard_map/ppermute | solution.py:15
  27.2 1.0 copy-start.7
  28.7 50.8 %copy-start.1 = (f32[256,256]{1,0:T(8,128)}, f32[256,256]{1,0:T(8,128)S(1)}, u32[]{:S(2)}) copy-start(f32[256,256]{1,0:T(8,128)S(1)} %fusion.45) | copy-start | bytes 786436
  28.7 1.0 copy-start.10
  30.1 49.4 %copy-start.11 = (f32[128,256]{1,0:T(8,128)S(1)}, f32[128,256]{1,0:T(8,128)}, u32[]{:S(2)}) copy-start(f32[128,256]{1,0:T(8,128)} %param.15) | copy-start | bytes 393220
  75.6 30.1 %all-to-all-start.1 = ((f32[32,1,3072]{2,1,0:T(1,128)}), f32[32,1,3072]{2,1,0:T(1,128)S(1)}, u32[]{:S(2)}, u32[]{:S(2)}) async-start(f32[32,1,3072]{2,1,0:T(1,128)} %broadcast_in_dim.11), calls=%async_computation.1 | async-start | bytes 786432 | tf_op jit(solution)/shard_map/all_to_all | solution.py:39
  110.3 17.7 %all-to-all-start.2 = ((f32[16,1,6144]{2,1,0:T(1,128)}), f32[16,1,6144]{2,1,0:T(1,128)S(1)}, u32[]{:S(2)}, u32[]{:S(2)}) async-start(f32[16,1,6144]{2,1,0:T(1,128)} %bitcast.16), calls=%async_computation.2 | async-start | bytes 786432 | tf_op jit(solution)/shard_map/all_to_all | solution.py:28
  129.2 14.2 %all-to-all-start.3 = ((f32[16,1,6144]{2,1,0:T(1,128)}), f32[16,1,6144]{2,1,0:T(1,128)S(1)}, u32[]{:S(2)}, u32[]{:S(2)}) async-start(f32[16,1,6144]{2,1,0:T(1,128)} %broadcast_in_dim.12), calls=%async_computation.3 | async-start | bytes 786432 | tf_op jit(solution)/shard_map/all_to_all | solution.py:39
  133.6 1.0 copy-start.2
  133.6 1.1 copy-start.3
  133.6 1.2 copy-start.4
  133.6 1.3 copy-start.5
  133.7 1.4 copy-start.6
where the time goes:
time: 147 us; the launch traced here: 146 us
  blocking collectives  44.3 us (30%)
  waiting for transfers between devices  42.9 us (29%)
  starting transfers between devices  29.6 us (20%)
  local copies, waits for them, and re-layouts  14.3 us (10%)
  other arithmetic  10.8 us (7%)
  matrix products  2.9 us (2%)
    all_to_all x1, blocking collectives, summed_on_arrival(): lax.all_to_all(pieces, axis, split_axis=0, concat_axis=0, tiled=True)  44.3 us
    all_to_all x2, waiting for transfers between devices, copy_for_each(): return lax.all_to_all(copies, axis, split_axis=0, concat_axis=0, tiled=True)  29.8 us
    all_to_all x1, waiting for transfers between devices, summed_on_arrival(): lax.all_to_all(pieces, axis, split_axis=0, concat_axis=0, tiled=True)  8.6 us
    all_to_all x2, starting transfers between devices, copy_for_each(): return lax.all_to_all(copies, axis, split_axis=0, concat_axis=0, tiled=True)  8.3 us
    all_to_all x1, starting transfers between devices, summed_on_arrival(): lax.all_to_all(pieces, axis, split_axis=0, concat_axis=0, tiled=True)  7.97 us
    ppermute x2, starting transfers between devices, with_halo(): lax.ppermute(lax.slice_in_dim(block, 0, width, axis=dim), axis, backward)  6.85 us
    ppermute x2, starting transfers between devices, with_halo(): lax.ppermute(lax.slice_in_dim(block, block.shape[dim] - width, None, axis...  6.45 us
    unnamed x31, local copies, waits for them, and re-layouts  5.83 us
  transfers between devices with their start and end apart: 7, of which 5 were waited for; matrix products, arithmetic and copies ran while one was open for 5% of the time, Pallas kernels for 0%

commit v1 on v0

v1 whole, which is shorter than its diff:
```python
import functools

import jax
import jax.numpy as jnp
from jax import lax
from jax.experimental import pallas as pl
from jax.experimental.pallas import tpu as pltpu
from jax.sharding import PartitionSpec as P

MESH = pl.DeviceIdType.MESH
F32 = jnp.float32
BF16 = jnp.bfloat16
NC = 16
NA = 32
NZ = 16
ALPHA = 0.25 / 12.0
CH = 32


def split(x):
    hi = x.astype(BF16)
    return hi, (x - hi.astype(F32)).astype(BF16)


def dot3(a, b):
    dot = functools.partial(jnp.dot, preferred_element_type=F32)
    (ah, al), (bh, bl) = a, b
    return dot(ah, bh) + (dot(ah, bl) + dot(al, bh))


def d12(f, axis):
    n = f.shape[axis]
    up1, dn1 = pltpu.roll(f, n - 1, axis), pltpu.roll(f, 1, axis)
    up2, dn2 = pltpu.roll(f, n - 2, axis), pltpu.roll(f, 2, axis)
    return 8.0 * (up1 - dn1) - (up2 - dn2)


def kernel(
    e_in, p_in, q_in, c_in, w_in, om_in, th_in, l_in, r_in,
    e_out, p_out, q_out, rng_out, cor_out, core_out,
    fld, wid, tsl, asl, bsl, xs, xb, sph, wpx, e1x, sv, shl, pv, qv,
    om, th, lm, rm, omh, thh, lmh, rmh, trh,
    rpart, cpart, kpart, rrec, crec, krec, zrec, rsum, csum, ksum, zsum,
    in_sem, out_sem, row_s, row_r, col_s, col_r, cor_s, cor_r,
    rs_s, rs_r, ag_s, ag_r,
):
    cross = lax.axis_index("cross")
    along = lax.axis_index("along")
    z, ylo = along // 2, along % 2
    plane = ylo * NC + cross

    loads = [
        pltpu.make_async_copy(src, fld.at[k, pl.ds(8, 256)], in_sem.at[k])
        for k, src in enumerate((e_in, p_in, q_in, c_in))
    ]
    loads.append(pltpu.make_async_copy(w_in, wid.at[pl.ds(8, 256)], in_sem.at[4]))
    for copy in loads:
        copy.start()
    mats = [
        pltpu.make_async_copy(src, dst, in_sem.at[5 + k])
        for k, (src, dst) in enumerate(((om_in, om), (th_in, th), (l_in, lm), (r_in, rm)))
    ]
    for copy in mats:
        copy.start()

    def along_peer(d):
        return {"cross": cross, "along": (along + d) % NA}

    def cross_peer(d):
        return {"cross": (cross + d) % NC, "along": along}

    def plane_peer(d):
        k = (plane + d) % NA
        return {"cross": k % NC, "along": z * 2 + k // NC}

    def z_peer(d):
        return {"cross": cross, "along": ((z + d) % NZ) * 2 + ylo}

    barrier = pltpu.get_barrier_semaphore()

    @pl.loop(1, NA)
    def _(d):
        pl.semaphore_signal(barrier, inc=1, device_id=along_peer(d), device_id_type=MESH)

    @pl.loop(1, NA)
    def _(d):
        pl.semaphore_signal(barrier, inc=1, device_id=plane_peer(d), device_id_type=MESH)

    for copy in loads:
        copy.wait()

    lane = lax.broadcasted_iota(jnp.int32, (128, 128), 1)
    for b in range(2):
        rows = pl.ds(8 + 128 * b, 128)
        fields = [wid[rows].astype(F32)] + [fld[k, rows] for k in (1, 2, 0, 3)]
        slab = jnp.zeros((128, 128), F32)
        for k, f in enumerate(fields):
            x = jnp.where(lane < 64, f[:, :128], f[:, 128:])
            x = pltpu.roll(x, 16 * k + 8, 1)
            slab = jnp.where((lane >= 16 * k) & (lane < 16 * k + 16), x, slab)
        tsl[:, :, :, pl.ds(128 * b, 128)] = slab.T.reshape(8, 2, 8, 128)

    @pl.when(along == NA - 1)
    def _():
        tsl[0, 0] = jnp.zeros((8, 256), F32)
        tsl[3, 0] = jnp.zeros((8, 256), F32)

    @pl.when(along == 0)
    def _():
        tsl[0, 1] = jnp.zeros((8, 256), F32)
        tsl[3, 1] = jnp.zeros((8, 256), F32)

    asl[5:8] = jnp.zeros((3, 2, 8, 256), F32)
    for side in range(2):
        bsl[side, 3:8] = jnp.zeros((5, 2, 8, 128), F32)

    pl.semaphore_wait(barrier, 2 * (NA - 1))

    halo = []
    for k in range(5):
        ref = wid if k == 4 else fld.at[k]
        for side, (src, dst, step) in enumerate(((256, 0, 1), (8, 264, NC - 1))):
            halo.append(
                pltpu.make_async_remote_copy(
                    src_ref=ref.at[pl.ds(src, 8)],
                    dst_ref=ref.at[pl.ds(dst, 8)],
                    send_sem=row_s.at[2 * k + side],
                    recv_sem=row_r.at[2 * k + side],
                    device_id=cross_peer(step),
                    device_id_type=MESH,
                )
            )
    cols = []
    for side, step in enumerate((1, NA - 1)):
        cols.append(
            pltpu.make_async_remote_copy(
                src_ref=tsl.at[pl.ds(0, 5), side],
                dst_ref=asl.at[pl.ds(0, 5), side],
                send_sem=col_s.at[side],
                recv_sem=col_r.at[side],
                device_id=along_peer(step),
                device_id_type=MESH,
            )
        )
    for copy in cols + halo:
        copy.start()

    for copy in mats:
        copy.wait()
    for src, dst in ((om, omh), (th, thh), (lm, lmh), (rm, rmh)):
        hi, lo = split(src[...])
        dst[0] = hi
        dst[1] = lo

    for copy in cols:
        copy.wait_recv()

    corners = []
    for side, step in enumerate((1, NC - 1)):
        corners.append(
            pltpu.make_async_remote_copy(
                src_ref=asl.at[pl.ds(0, 3), :, :, pl.ds(128 * (1 - side), 128)],
                dst_ref=bsl.at[side, pl.ds(0, 3)],
                send_sem=cor_s.at[side],
                recv_sem=cor_r.at[side],
                device_id=cross_peer(step),
                device_id_type=MESH,
            )
        )
    for copy in corners:
        copy.start()

    for b in range(2):
        xs[pl.ds(128 * b, 128)] = asl[:, :, :, pl.ds(128 * b, 128)].reshape(128, 128).T

    for copy in halo:
        copy.wait_recv()

    @pl.when(cross == 0)
    def _():
        fld[0, pl.ds(0, 8)] = jnp.zeros((8, 256), F32)
        wid[pl.ds(0, 8)] = jnp.zeros((8, 256), jnp.int32)

    @pl.when(cross == NC - 1)
    def _():
        fld[0, pl.ds(264, 8)] = jnp.zeros((8, 256), F32)
        wid[pl.ds(264, 8)] = jnp.zeros((8, 256), jnp.int32)

    def beside(x, k):
        return pltpu.roll(x, 128 - (16 * k + 8), 1)

    def sp_rows(r, n, lead):
        w = wid[pl.ds(r, n)].astype(F32)
        wp = w * fld[1, pl.ds(r, n)]
        c = fld[3, pl.ds(r, n)]
        e = fld[0, pl.ds(pl.multiple_of(r - lead, 8), n + 16)]
        de = d12(e, 0)[lead : lead + n]
        wpx[pl.ds(r, n)] = wp
        sph[pl.ds(r, n)] = 2.0 * wp - w * c * ALPHA * de - (0.02 / c) * wp

    @pl.loop(0, 256 // CH)
    def _(i):
        sp_rows(pl.multiple_of(8 + i * CH, 8), CH, 8)

    sp_rows(0, 8, 0)
    sp_rows(264, 8, 16)

    @pl.loop(0, 256 // CH)
    def _(i):
        r0 = pl.multiple_of(i * CH, 8)
        r = pl.multiple_of(8 + i * CH, 8)
        own = pl.ds(r, CH)
        x = xs[pl.ds(r0, CH)]
        wt = wid[own].astype(F32)
        e0 = fld[0, own]
        w = jnp.concatenate([wt, beside(x, 0)], axis=1)
        q = jnp.concatenate([fld[2, own], beside(x, 2)], axis=1)
        e = jnp.concatenate([e0, beside(x, 3)], axis=1)
        c = jnp.concatenate([fld[3, own], beside(x, 4)], axis=1)
        wq = w * q
        sq = 2.0 * wq - w * c * ALPHA * d12(e, 1) - (0.02 / c) * wq
        dy = d12(sq, 1)[:, :256]
        s = sph[pl.ds(pl.multiple_of(r - 8, 8), CH + 16)]
        dx = d12(s, 0)[8 : 8 + CH]
        en = e0 - (0.5 * ALPHA) * wt * (dx + dy)
        sv[pl.ds(r0, CH)] = en
        hi, lo = split(en)
        shl[0, pl.ds(r0, CH)] = hi
        shl[1, pl.ds(r0, CH)] = lo

    outs = [pltpu.make_async_copy(sv, e_out, out_sem.at[0])]
    outs[0].start()

    def send(n, peer, src, dst, phase, s_sem, r_sem):
        @pl.loop(0, n - 1)
        def _(s):
            half = (s + 1) // 2
            d = n // 2 + (1 - 2 * (s % 2)) * half
            pltpu.make_async_remote_copy(
                src_ref=src(d),
                dst_ref=dst(d),
                send_sem=s_sem.at[phase],
                recv_sem=r_sem.at[phase],
                device_id=peer(d),
                device_id_type=MESH,
            ).start()

    def await_recv(ref, sem):
        pltpu.make_async_copy(ref, ref, sem).wait()

    surf = (shl[0], shl[1])
    rpart[...] = dot3(surf, (omh[0], omh[1])).reshape(NA, 8, 128)
    send(NA, along_peer, lambda d: rpart.at[(along + d) % NA], lambda d: rrec.at[d], 0, rs_s, rs_r)
    tr = dot3(surf, (rmh[0], rmh[1]))
    hi, lo = split(tr)
    trh[0] = hi
    trh[1] = lo
    kpart[...] = dot3((lmh[0], lmh[1]), (trh[0], trh[1])).reshape(NA, 8, 256)
    send(NA, plane_peer, lambda d: kpart.at[(plane + d) % NA], lambda d: krec.at[d], 1, rs_s, rs_r)
    cpart[...] = dot3((thh[0], thh[1]), surf).reshape(NC, 8, 256)
    send(NC, cross_peer, lambda d: cpart.at[(cross + d) % NC], lambda d: crec.at[d], 2, rs_s, rs_r)

    for copy in corners:
        copy.wait_recv()

    @pl.when(cross == 0)
    def _():
        bsl[0] = jnp.zeros((8, 2, 8, 128), F32)

    @pl.when(cross == NC - 1)
    def _():
        bsl[1] = jnp.zeros((8, 2, 8, 128), F32)

    for side in range(2):
        t = bsl[side, pl.ds(0, 8)].reshape(128, 128).T
        xb[pl.ds(8 * side, 8)] = t[120:128] if side == 0 else t[0:8]

    def e1_rows(r, n, x, lead):
        w = wid[pl.ds(r, n)].astype(F32)
        wq = jnp.concatenate(
            [w * fld[2, pl.ds(r, n)], beside(x, 0) * beside(x, 2)], axis=1
        )
        wp = wpx[pl.ds(pl.multiple_of(r - lead, 8), n + 16)]
        dx = d12(wp, 0)[lead : lead + n]
        dy = d12(wq, 1)[:, :256]
        e = fld[0, pl.ds(r, n)]
        return e + (e - ALPHA * w * (dx + dy))

    @pl.loop(0, 256 // CH)
    def _(i):
        r = pl.multiple_of(8 + i * CH, 8)
        e1x[pl.ds(r, CH)] = e1_rows(r, CH, xs[pl.ds(pl.multiple_of(i * CH, 8), CH)], 8)

    e1x[pl.ds(0, 8)] = e1_rows(0, 8, xb[pl.ds(0, 8)], 0)
    e1x[pl.ds(264, 8)] = e1_rows(264, 8, xb[pl.ds(8, 8)], 16)

    xb[pl.ds(16, 256)] = xs[...]

    @pl.loop(0, 256 // CH)
    def _(i):
        r0 = pl.multiple_of(i * CH, 8)
        r = pl.multiple_of(8 + i * CH, 8)
        own = pl.ds(r, CH)
        x = xs[pl.ds(r0, CH)]
        w = wid[own].astype(F32)
        c = fld[3, own]
        p, q = fld[1, own], fld[2, own]
        wc = w * c * ALPHA
        fr = w * (0.02 / c)
        p1 = p - wc * d12(fld[0, pl.ds(r0, CH + 16)], 0)[8 : 8 + CH] - fr * p
        ee = e1x[pl.ds(r0, CH + 16)]
        dx = d12(ee, 0)[8 : 8 + CH]
        pv[pl.ds(r0, CH)] = p - 0.5 * (wc * dx + fr * (p + p1))

        hb = jnp.concatenate(
            [
                jnp.where(i == 0, xb[pl.ds(0, 8)], xb[pl.ds(pl.multiple_of(jnp.maximum(r0 + 8, 8), 8), 8)]),
                x,
                jnp.where(
                    i == 256 // CH - 1,
                    xb[pl.ds(8, 8)],
                    xb[pl.ds(pl.multiple_of(jnp.minimum(r0 + 16 + CH, 264), 8), 8)],
                ),
            ],
            axis=0,
        )
        wpb = beside(hb, 0) * beside(hb, 1)
        dxb = d12(wpb, 0)[8 : 8 + CH]
        wb = beside(x, 0)
        wq = jnp.concatenate([w * q, wb * beside(x, 2)], axis=1)
        dyb = d12(wq, 1)[:, 256:]
        eb = beside(x, 3)
        e1b = eb + (eb - ALPHA * wb * (dxb + dyb))
        e = jnp.concatenate([fld[0, own], eb], axis=1)
        q1 = q - wc * d12(e, 1)[:, :256] - fr * q
        dy = d12(jnp.concatenate([e1x[own], e1b], axis=1), 1)[:, :256]
        qv[pl.ds(r0, CH)] = q - 0.5 * (wc * dy + fr * (q + q1))

    outs += [
        pltpu.make_async_copy(pv, p_out, out_sem.at[1]),
        pltpu.make_async_copy(qv, q_out, out_sem.at[2]),
    ]
    outs[1].start()
    outs[2].start()

    await_recv(krec.at[pl.ds(1, NA - 1)], rs_r.at[1])
    krec[0] = kpart[plane]
    ksum[...] = jnp.sum(krec[...], axis=0)
    send(NZ, z_peer, lambda d: ksum, lambda d: zrec.at[d], 3, rs_s, rs_r)

    await_recv(crec.at[pl.ds(1, NC - 1)], rs_r.at[2])
    crec[0] = cpart[cross]
    csum[pl.ds(pl.multiple_of(8 * cross, 8), 8)] = jnp.sum(crec[...], axis=0)
    mine = pl.ds(pl.multiple_of(8 * cross, 8), 8)
    send(NC, cross_peer, lambda d: csum.at[mine], lambda d: csum.at[mine], 2, ag_s, ag_r)

    await_recv(rrec.at[pl.ds(1, NA - 1)], rs_r.at[0])
    rrec[0] = rpart[along]
    own_r = pl.ds(pl.multiple_of(8 * along, 8), 8)
    rsum[own_r] = jnp.sum(rrec[...], axis=0)
    send(NA, along_peer, lambda d: rsum.at[own_r], lambda d: rsum.at[own_r], 0, ag_s, ag_r)

    await_recv(zrec.at[pl.ds(1, NZ - 1)], rs_r.at[3])
    zrec[0] = ksum[...]
    total = zrec[z]
    for k in range(1, NZ):
        total = total + zrec[(z - k + NZ) % NZ]
    own_k = pl.ds(pl.multiple_of(8 * plane, 8), 8)
    zsum[own_k] = total
    send(NA, plane_peer, lambda d: zsum.at[own_k], lambda d: zsum.at[own_k], 1, ag_s, ag_r)

    await_recv(csum.at[pl.ds(0, 120)], ag_r.at[2])
    outs.append(pltpu.make_async_copy(csum, cor_out, out_sem.at[4]))
    outs[-1].start()
    await_recv(rsum.at[pl.ds(0, 248)], ag_r.at[0])
    outs.append(pltpu.make_async_copy(rsum, rng_out, out_sem.at[3]))
    outs[-1].start()
    await_recv(zsum.at[pl.ds(0, 248)], ag_r.at[1])
    outs.append(pltpu.make_async_copy(zsum, core_out, out_sem.at[5]))
    outs[-1].start()

    for copy in halo + cols + corners:
        copy.wait_send()
    await_recv(rrec.at[pl.ds(1, NA - 1)], rs_s.at[0])
    await_recv(krec.at[pl.ds(1, NA - 1)], rs_s.at[1])
    await_recv(crec.at[pl.ds(1, NC - 1)], rs_s.at[2])
    await_recv(zrec.at[pl.ds(1, NZ - 1)], rs_s.at[3])
    await_recv(rsum.at[pl.ds(0, 248)], ag_s.at[0])
    await_recv(zsum.at[pl.ds(0, 248)], ag_s.at[1])
    await_recv(csum.at[pl.ds(0, 120)], ag_s.at[2])
    for copy in outs:
        copy.wait()


def body(*args):
    vm = pltpu.VMEM
    dma = pltpu.SemaphoreType.DMA
    sds = jax.ShapeDtypeStruct
    return pl.pallas_call(
        kernel,
        out_shape=(
            sds((256, 256), F32),
            sds((256, 256), F32),
            sds((256, 256), F32),
            sds((256, 128), F32),
            sds((128, 256), F32),
            sds((256, 256), F32),
        ),
        in_specs=[pl.BlockSpec(memory_space=pl.ANY)] * 9,
        out_specs=[pl.BlockSpec(memory_space=pl.ANY)] * 6,
        scratch_shapes=[
            vm((4, 272, 256), F32),
            vm((272, 256), jnp.int32),
            vm((8, 2, 8, 256), F32),
            vm((8, 2, 8, 256), F32),
            vm((2, 8, 2, 8, 128), F32),
            vm((256, 128), F32),
            vm((272, 128), F32),
            vm((272, 256), F32),
            vm((272, 256), F32),
            vm((272, 256), F32),
            vm((256, 256), F32),
            vm((2, 256, 256), BF16),
            vm((256, 256), F32),
            vm((256, 256), F32),
            vm((256, 128), F32),
            vm((128, 256), F32),
            vm((256, 256), F32),
            vm((256, 256), F32),
            vm((2, 256, 128), BF16),
            vm((2, 128, 256), BF16),
            vm((2, 256, 256), BF16),
            vm((2, 256, 256), BF16),
            vm((2, 256, 256), BF16),
            vm((NA, 8, 128), F32),
            vm((NC, 8, 256), F32),
            vm((NA, 8, 256), F32),
            vm((NA, 8, 128), F32),
            vm((NC, 8, 256), F32),
            vm((NA, 8, 256), F32),
            vm((NZ, 8, 256), F32),
            vm((256, 128), F32),
            vm((128, 256), F32),
            vm((8, 256), F32),
            vm((256, 256), F32),
            dma((9,)),
            dma((6,)),
            dma((10,)),
            dma((10,)),
            dma((2,)),
            dma((2,)),
            dma((2,)),
            dma((2,)),
            dma((4,)),
            dma((4,)),
            dma((3,)),
            dma((3,)),
        ],
        compiler_params=pltpu.CompilerParams(collective_id=0, has_side_effects=True),
    )(*args)


def solution(mesh):
    return jax.shard_map(
        body,
        mesh=mesh,
        in_specs=(
            P("cross", "along"),
            P("cross", "along"),
            P("cross", "along"),
            P("cross", "along"),
            P("cross", "along"),
            P("along", None),
            P(None, "cross"),
            P(None, "cross"),
            P("along", None),
        ),
        out_specs=(
            P("cross", "along"),
            P("cross", "along"),
            P("cross", "along"),
            P("cross", None),
            P(None, "along"),
            P(),
        ),
        check_vma=False,
    )
```

time: 147 us -> 56.5 us (0.38)
  Pallas kernels: 0 us -> 49.9 us
  blocking collectives: 44.3 us -> 0 us
  waiting for transfers between devices: 42.9 us -> 0 us
  starting transfers between devices: 29.6 us -> 0 us
  other arithmetic: 10.8 us -> 0 us
  local copies, waits for them, and re-layouts: 14.3 us -> 5.77 us
  matrix products: 2.9 us -> 0 us
    pallas_call x0 -> x1, Pallas kernels: none -> 49.9 us  [body(): pl.pallas_call(kernel, out_shape=(sds((256, 256), F32), sds((256, 256), F...]
    all_to_all x1 -> x0, blocking collectives: 44.3 us -> none  [summed_on_arrival(): lax.all_to_all(pieces, axis, split_axis=0, concat_axis=0, tiled=True)]
    all_to_all x3 -> x0, waiting for transfers between devices: 38.4 us -> none  [the longest x2 29.8 us: copy_for_each(): return lax.all_to_all(copies, axis, split_axis=0, concat_axis=0, tiled=True)]
    all_to_all x3 -> x0, starting transfers between devices: 16.3 us -> none  [the longest x2 8.3 us: copy_for_each(): return lax.all_to_all(copies, axis, split_axis=0, concat_axis=0, tiled=True)]
    ppermute x4 -> x0, starting transfers between devices: 13.3 us -> none  [the longest x2 6.85 us: with_halo(): lax.ppermute(lax.slice_in_dim(block, 0, width, axis=dim), axis, backward)]
    slice x16 -> x0, local copies, waits for them, and re-layouts: 5.7 us -> none  [the longest x7 2.61 us: part(): return lax.slice_in_dim(padded, start, start + count, axis=axis)]
    ppermute x4 -> x0, waiting for transfers between devices: 4.47 us -> none  [the longest x2 4.47 us: with_halo(): lax.ppermute(lax.slice_in_dim(block, 0, width, axis=dim), axis, backward)]
    add x3 -> x0, other arithmetic: 3.91 us -> none  [the longest x1 2.62 us: body(): flux_along_next = flux_along + 0.5 * (k1q + k2q)]
  transfers between devices with their start and end apart: 7 -> 0, of which waited for: 5 -> 0; matrix products, arithmetic and copies ran while one was open for 5% -> 0% of each run, Pallas kernels for 0% -> 0%
where the time goes in v1:
time: 56.5 us; the launch traced here: 56.3 us
  Pallas kernels  49.9 us (88%)
  local copies, waits for them, and re-layouts  5.77 us (10%)
  between operations  0.66 us (1%)
    pallas_call x1, Pallas kernels, body(): pl.pallas_call(kernel, out_shape=(sds((256, 256), F32), sds((256, 256), F...  49.9 us
    unnamed x16, local copies, waits for them, and re-layouts  5.77 us

profile of v1, /device:TPU:1, one launch (start us, length us, event | category | flops | bytes accessed | tf_op | source)
XLA Modules:
  0.0 56.3 jit_solution(6629734127685685002)
XLA Ops:
  0.6 49.9 %shard_map.136 = (f32[256,256]{1,0:T(8,128)}, f32[256,256]{1,0:T(8,128)}, f32[256,256]{1,0:T(8,128)}, f32[256,128]{1,0:T(8,128)}, f32[128,256]{1,0:T(8,128)}, /*index=5*/f32[256,256]{1,0:T(8,128)}) custom-call(f32[256,256]{1,0:T(8,128)} %e_in.1, f32[256,256]{1,0:T(8,128)} %p_in.1, f32[256,256]{1,0:T(8,128)} %q_in.1, f32[256,256]{1,0:T(8,128)} %c_in.1, ...), custom_call_target="tpu_custom_call" | custom-call | tf_op jit(solution)/shard_map/pallas_call | solution.py:399
  50.5 0.0 copy-start.2
  50.5 1.7 %copy.21 = f32[256,256]{1,0:T(8,128)} copy(f32[256,256]{1,0:T(8,128)} %get-tuple-element.12) | data formatting | bytes 524288
  52.2 0.0 copy-done.2
  52.2 0.0 copy-start.1
  52.2 0.7 %copy.22 = f32[256,256]{1,0:T(8,128)} copy(f32[256,256]{1,0:T(8,128)S(1)} %copy-done.2) | data formatting | bytes 524288
  52.9 0.3 copy-done.1
  53.3 0.0 copy-start.4
  53.3 0.0 copy-start.3
  53.3 0.7 %copy.23 = f32[256,256]{1,0:T(8,128)} copy(f32[256,256]{1,0:T(8,128)S(1)} %copy-done.1) | data formatting | bytes 524288
  54.0 0.3 copy-done.4
  54.3 0.0 copy-start
  54.3 0.7 %copy.24 = f32[256,128]{1,0:T(8,128)} copy(f32[256,128]{1,0:T(8,128)S(1)} %copy-done.4) | data formatting | bytes 262144
  54.9 0.0 copy-done.3
  54.9 0.7 %copy.25 = f32[128,256]{1,0:T(8,128)} copy(f32[128,256]{1,0:T(8,128)S(1)} %copy-done.3) | data formatting | bytes 262144
  55.6 0.0 copy-done
  55.6 0.7 %copy.26 = f32[256,256]{1,0:T(8,128)} copy(f32[256,256]{1,0:T(8,128)S(1)} %copy-done) | data formatting | bytes 524288
Async XLA Ops:
  50.5 1.7 %copy-start.2 = (f32[256,256]{1,0:T(8,128)S(1)}, f32[256,256]{1,0:T(8,128)}, u32[]{:S(2)}) copy-start(f32[256,256]{1,0:T(8,128)} %get-tuple-element.13) | copy-start | bytes 786436
  52.2 1.0 %copy-start.1 = (f32[256,256]{1,0:T(8,128)S(1)}, f32[256,256]{1,0:T(8,128)}, u32[]{:S(2)}) copy-start(f32[256,256]{1,0:T(8,128)} %get-tuple-element.14) | copy-start | bytes 786436
  53.3 1.0 %copy-start.4 = (f32[256,128]{1,0:T(8,128)S(1)}, f32[256,128]{1,0:T(8,128)}, u32[]{:S(2)}) copy-start(f32[256,128]{1,0:T(8,128)} %get-tuple-element.15) | copy-start | bytes 393220
  53.3 1.7 %copy-start.3 = (f32[128,256]{1,0:T(8,128)S(1)}, f32[128,256]{1,0:T(8,128)}, u32[]{:S(2)}) copy-start(f32[128,256]{1,0:T(8,128)} %get-tuple-element.16) | copy-start | bytes 393220
  54.3 1.3 %copy-start = (f32[256,256]{1,0:T(8,128)S(1)}, f32[256,256]{1,0:T(8,128)}, u32[]{:S(2)}) copy-start(f32[256,256]{1,0:T(8,128)} %get-tuple-element.17) | copy-start | bytes 786436

commit v2 on v1

--- a/solution.py
+++ b/solution.py
@@ -37,12 +37,12 @@
 
 def kernel(
     e_in, p_in, q_in, c_in, w_in, om_in, th_in, l_in, r_in,
-    e_out, p_out, q_out, rng_out, cor_out, core_out,
-    fld, wid, tsl, asl, bsl, xs, xb, sph, wpx, e1x, sv, shl, pv, qv,
-    om, th, lm, rm, omh, thh, lmh, rmh, trh,
-    rpart, cpart, kpart, rrec, crec, krec, zrec, rsum, csum, ksum, zsum,
-    in_sem, out_sem, row_s, row_r, col_s, col_r, cor_s, cor_r,
-    rs_s, rs_r, ag_s, ag_r,
+    sv, pv, qv, rsum, csum, zsum,
+    fld, wid, tsl, asl, bsl, xs, xb, sph, wpx, e1x, shl,
+    om, th, lm, rm, omh, thh, lmh, rmh,
+    rpart, cpart, kpart, rrec, crec, krec, zrec, ksum,
+    in_sem, row_s, row_r, col_s, col_r, cor_s, cor_r,
+    rs_s, rs_r, ag_s, ag_r, near,
 ):
     cross = lax.axis_index("cross")
     along = lax.axis_index("along")
@@ -63,28 +63,39 @@
     for copy in mats:
         copy.start()
 
+    rem = lax.rem
+
     def along_peer(d):
-        return {"cross": cross, "along": (along + d) % NA}
+        return {"cross": cross, "along": rem(along + d, NA)}
 
     def cross_peer(d):
-        return {"cross": (cross + d) % NC, "along": along}
+        return {"cross": rem(cross + d, NC), "along": along}
 
     def plane_peer(d):
-        k = (plane + d) % NA
-        return {"cross": k % NC, "along": z * 2 + k // NC}
-
-    def z_peer(d):
-        return {"cross": cross, "along": ((z + d) % NZ) * 2 + ylo}
+        k = rem(plane + d, NA)
+        return {"cross": rem(k, NC), "along": z * 2 + lax.div(k, NC)}
+
+    def z_peer(d, y=ylo):
+        return {"cross": cross, "along": rem(z + d, NZ) * 2 + y}
+
+    def signal(sem, peer):
+        pl.semaphore_signal(sem, inc=1, device_id=peer, device_id_type=MESH)
 
     barrier = pltpu.get_barrier_semaphore()
+    for d in (1, NZ - 1):
+        for y in range(2):
+            signal(barrier, z_peer(d, y))
 
     @pl.loop(1, NA)
     def _(d):
-        pl.semaphore_signal(barrier, inc=1, device_id=along_peer(d), device_id_type=MESH)
-
-    @pl.loop(1, NA)
-    def _(d):
-        pl.semaphore_signal(barrier, inc=1, device_id=plane_peer(d), device_id_type=MESH)
+        signal(barrier, plane_peer(d))
+
+    def tell(k):
+        for d in (2**k, NZ - 2**k):
+            signal(near.at[k], z_peer(d))
+
+    def hear(k):
+        pl.semaphore_wait(near.at[k], 2)
 
     for copy in loads:
         copy.wait()
@@ -114,7 +125,8 @@
     for side in range(2):
         bsl[side, 3:8] = jnp.zeros((5, 2, 8, 128), F32)
 
-    pl.semaphore_wait(barrier, 2 * (NA - 1))
+    pl.semaphore_wait(barrier, NA - 1 + 4)
+    tell(0)
 
     halo = []
     for k in range(5):
@@ -173,6 +185,8 @@
     for b in range(2):
         xs[pl.ds(128 * b, 128)] = asl[:, :, :, pl.ds(128 * b, 128)].reshape(128, 128).T
 
+    hear(0)
+    tell(1)
     for copy in halo:
         copy.wait_recv()
 
@@ -204,6 +218,8 @@
 
     sp_rows(0, 8, 0)
     sp_rows(264, 8, 16)
+    hear(1)
+    tell(2)
 
     @pl.loop(0, 256 // CH)
     def _(i):
@@ -228,14 +244,8 @@
         shl[0, pl.ds(r0, CH)] = hi
         shl[1, pl.ds(r0, CH)] = lo
 
-    outs = [pltpu.make_async_copy(sv, e_out, out_sem.at[0])]
-    outs[0].start()
-
     def send(n, peer, src, dst, phase, s_sem, r_sem):
-        @pl.loop(0, n - 1)
-        def _(s):
-            half = (s + 1) // 2
-            d = n // 2 + (1 - 2 * (s % 2)) * half
+        def one(d):
             pltpu.make_async_remote_copy(
                 src_ref=src(d),
                 dst_ref=dst(d),
@@ -245,20 +255,25 @@
                 device_id_type=MESH,
             ).start()
 
+        one(n // 2)
+
+        @pl.loop(1, n // 2)
+        def _(s):
+            one(n // 2 - s)
+            one(n // 2 + s)
+
     def await_recv(ref, sem):
         pltpu.make_async_copy(ref, ref, sem).wait()
 
     surf = (shl[0], shl[1])
+    tr = dot3(surf, (rmh[0], rmh[1]))
+    kpart[...] = dot3((lmh[0], lmh[1]), split(tr)).reshape(NA, 8, 256)
+    send(NA, plane_peer, lambda d: kpart.at[rem(plane + d, NA)], lambda d: krec.at[d], 1, rs_s, rs_r)
     rpart[...] = dot3(surf, (omh[0], omh[1])).reshape(NA, 8, 128)
-    send(NA, along_peer, lambda d: rpart.at[(along + d) % NA], lambda d: rrec.at[d], 0, rs_s, rs_r)
-    tr = dot3(surf, (rmh[0], rmh[1]))
-    hi, lo = split(tr)
-    trh[0] = hi
-    trh[1] = lo
-    kpart[...] = dot3((lmh[0], lmh[1]), (trh[0], trh[1])).reshape(NA, 8, 256)
-    send(NA, plane_peer, lambda d: kpart.at[(plane + d) % NA], lambda d: krec.at[d], 1, rs_s, rs_r)
+    hear(2)
+    send(NA, along_peer, lambda d: rpart.at[rem(along + d, NA)], lambda d: rrec.at[d], 0, rs_s, rs_r)
     cpart[...] = dot3((thh[0], thh[1]), surf).reshape(NC, 8, 256)
-    send(NC, cross_peer, lambda d: cpart.at[(cross + d) % NC], lambda d: crec.at[d], 2, rs_s, rs_r)
+    send(NC, cross_peer, lambda d: cpart.at[rem(cross + d, NC)], lambda d: crec.at[d], 2, rs_s, rs_r)
 
     for copy in corners:
         copy.wait_recv()
@@ -336,13 +351,6 @@
         dy = d12(jnp.concatenate([e1x[own], e1b], axis=1), 1)[:, :256]
         qv[pl.ds(r0, CH)] = q - 0.5 * (wc * dy + fr * (q + q1))
 
-    outs += [
-        pltpu.make_async_copy(pv, p_out, out_sem.at[1]),
-        pltpu.make_async_copy(qv, q_out, out_sem.at[2]),
-    ]
-    outs[1].start()
-    outs[2].start()
-
     await_recv(krec.at[pl.ds(1, NA - 1)], rs_r.at[1])
     krec[0] = kpart[plane]
     ksum[...] = jnp.sum(krec[...], axis=0)
@@ -356,39 +364,50 @@
 
     await_recv(rrec.at[pl.ds(1, NA - 1)], rs_r.at[0])
     rrec[0] = rpart[along]
-    own_r = pl.ds(pl.multiple_of(8 * along, 8), 8)
-    rsum[own_r] = jnp.sum(rrec[...], axis=0)
-    send(NA, along_peer, lambda d: rsum.at[own_r], lambda d: rsum.at[own_r], 0, ag_s, ag_r)
+    rsum[z, ylo] = jnp.sum(rrec[...], axis=0)
+    own_r = rsum.at[z, ylo]
+    send(NZ, z_peer, lambda d: own_r, lambda d: own_r, 0, ag_s, ag_r)
 
     await_recv(zrec.at[pl.ds(1, NZ - 1)], rs_r.at[3])
     zrec[0] = ksum[...]
     total = zrec[z]
     for k in range(1, NZ):
-        total = total + zrec[(z - k + NZ) % NZ]
+        total = total + zrec[rem(z - k + NZ, NZ)]
     own_k = pl.ds(pl.multiple_of(8 * plane, 8), 8)
     zsum[own_k] = total
     send(NA, plane_peer, lambda d: zsum.at[own_k], lambda d: zsum.at[own_k], 1, ag_s, ag_r)
 
     await_recv(csum.at[pl.ds(0, 120)], ag_r.at[2])
-    outs.append(pltpu.make_async_copy(csum, cor_out, out_sem.at[4]))
-    outs[-1].start()
-    await_recv(rsum.at[pl.ds(0, 248)], ag_r.at[0])
-    outs.append(pltpu.make_async_copy(rsum, rng_out, out_sem.at[3]))
-    outs[-1].start()
+    await_recv(rsum.at[pl.ds(0, NZ - 1), 0], ag_r.at[0])
+    pair = pltpu.make_async_remote_copy(
+        src_ref=rsum.at[:, ylo],
+        dst_ref=rsum.at[:, ylo],
+        send_sem=ag_s.at[3],
+        recv_sem=ag_r.at[3],
+        device_id={"cross": cross, "along": z * 2 + 1 - ylo},
+        device_id_type=MESH,
+    )
+    pair.start()
     await_recv(zsum.at[pl.ds(0, 248)], ag_r.at[1])
-    outs.append(pltpu.make_async_copy(zsum, core_out, out_sem.at[5]))
-    outs[-1].start()
-
-    for copy in halo + cols + corners:
+    pair.wait_recv()
+
+    for copy in halo + cols + corners + [pair]:
         copy.wait_send()
     await_recv(rrec.at[pl.ds(1, NA - 1)], rs_s.at[0])
     await_recv(krec.at[pl.ds(1, NA - 1)], rs_s.at[1])
     await_recv(crec.at[pl.ds(1, NC - 1)], rs_s.at[2])
     await_recv(zrec.at[pl.ds(1, NZ - 1)], rs_s.at[3])
-    await_recv(rsum.at[pl.ds(0, 248)], ag_s.at[0])
+    await_recv(rsum.at[pl.ds(0, NZ - 1), 0], ag_s.at[0])
     await_recv(zsum.at[pl.ds(0, 248)], ag_s.at[1])
     await_recv(csum.at[pl.ds(0, 120)], ag_s.at[2])
-    for copy in outs:
+
+
+def write_out(*refs):
+    ins, outs, sem = refs[:6], refs[6:12], refs[12]
+    copies = [pltpu.make_async_copy(a, b, sem.at[k]) for k, (a, b) in enumerate(zip(ins, outs))]
+    for copy in copies:
+        copy.start()
+    for copy in copies:
         copy.wait()
 
 
@@ -396,18 +415,18 @@
     vm = pltpu.VMEM
     dma = pltpu.SemaphoreType.DMA
     sds = jax.ShapeDtypeStruct
-    return pl.pallas_call(
+    held = pl.pallas_call(
         kernel,
         out_shape=(
             sds((256, 256), F32),
             sds((256, 256), F32),
             sds((256, 256), F32),
-            sds((256, 128), F32),
+            sds((NZ, 2, 8, 128), F32),
             sds((128, 256), F32),
             sds((256, 256), F32),
         ),
         in_specs=[pl.BlockSpec(memory_space=pl.ANY)] * 9,
-        out_specs=[pl.BlockSpec(memory_space=pl.ANY)] * 6,
+        out_specs=[pl.BlockSpec(memory_space=pltpu.VMEM)] * 6,
         scratch_shapes=[
             vm((4, 272, 256), F32),
             vm((272, 256), jnp.int32),
@@ -419,17 +438,13 @@
             vm((272, 256), F32),
             vm((272, 256), F32),
             vm((272, 256), F32),
-            vm((256, 256), F32),
             vm((2, 256, 256), BF16),
-            vm((256, 256), F32),
-            vm((256, 256), F32),
             vm((256, 128), F32),
             vm((128, 256), F32),
             vm((256, 256), F32),
             vm((256, 256), F32),
             vm((2, 256, 128), BF16),
             vm((2, 128, 256), BF16),
-            vm((2, 256, 256), BF16),
             vm((2, 256, 256), BF16),
             vm((2, 256, 256), BF16),
             vm((NA, 8, 128), F32),
@@ -439,12 +454,8 @@
             vm((NC, 8, 256), F32),
             vm((NA, 8, 256), F32),
             vm((NZ, 8, 256), F32),
-            vm((256, 128), F32),
-            vm((128, 256), F32),
             vm((8, 256), F32),
-            vm((256, 256), F32),
             dma((9,)),
-            dma((6,)),
             dma((10,)),
             dma((10,)),
             dma((2,)),
@@ -453,11 +464,21 @@
             dma((2,)),
             dma((4,)),
             dma((4,)),
-            dma((3,)),
-            dma((3,)),
+            dma((4,)),
+            dma((4,)),
+            pltpu.SemaphoreType.REGULAR((3,)),
         ],
-        compiler_params=pltpu.CompilerParams(collective_id=0, has_side_effects=True),
-    )(*args)
+        compiler_params=pltpu.CompilerParams(collective_id=0, has_side_effects=True, vmem_limit_bytes=16 << 20),
+    )(*[pltpu.with_memory_space_constraint(a, pltpu.HBM) for a in args])
+    held = held[:3] + (held[3].reshape(256, 128),) + held[4:]
+    return pl.pallas_call(
+        write_out,
+        out_shape=tuple(sds(x.shape, F32) for x in held),
+        in_specs=[pl.BlockSpec(memory_space=pltpu.VMEM)] * 6,
+        out_specs=[pl.BlockSpec(memory_space=pl.ANY)] * 6,
+        scratch_shapes=[dma((6,))],
+        compiler_params=pltpu.CompilerParams(vmem_limit_bytes=8 << 20),
+    )(*held)
 
 
 def solution(mesh):

time: 56.5 us -> 48.5 us (0.86)
  local copies, waits for them, and re-layouts: 5.77 us -> 0 us
  Pallas kernels: 49.9 us -> 47.8 us
    unnamed x16 -> x0, local copies, waits for them, and re-layouts: 5.77 us -> none
    pallas_call x1, Pallas kernels: 49.9 us -> 46.7 us  [body(): pl.pallas_call(kernel, out_shape=(sds((256, 256), F32), sds((256, 256), F...]
    pallas_call x0 -> x1, Pallas kernels: none -> 1.1 us  [body(): pl.pallas_call(write_out, out_shape=tuple((sds(x.shape, F32) for x in hel...]
where the time goes in v2:
time: 48.5 us; the launch traced here: 48.4 us
  Pallas kernels  47.8 us (99%)
  between operations  0.64 us (1%)
    pallas_call x1, Pallas kernels, body(): pl.pallas_call(kernel, out_shape=(sds((256, 256), F32), sds((256, 256), F...  46.7 us
    pallas_call x1, Pallas kernels, body(): pl.pallas_call(write_out, out_shape=tuple((sds(x.shape, F32) for x in hel...  1.1 us

profile of v2, /device:TPU:1, one launch (start us, length us, event | category | flops | bytes accessed | tf_op | source)
XLA Modules:
  0.0 48.4 jit_solution(10864885527846632133)
XLA Ops:
  0.6 46.7 %shard_map.136 = (f32[256,256]{1,0:T(8,128)S(1)}, f32[256,256]{1,0:T(8,128)S(1)}, f32[256,256]{1,0:T(8,128)S(1)}, f32[16,2,8,128]{3,2,1,0:T(8,128)S(1)}, f32[128,256]{1,0:T(8,128)S(1)}, /*index=5*/f32[256,256]{1,0:T(8,128)S(1)}) custom-call(f32[256,256]{1,0:T(8,128)} %e_in.1, f32[256,256]{1,0:T(8,128)} %p_in.1, f32[256,256]{1,0:T(8,128)} %q_in.1, ...), custom_call_target="tpu_custom_call" | custom-call | tf_op jit(solution)/shard_map/pallas_call | solution.py:418
  47.3 1.1 %shard_map.137 = (f32[256,256]{1,0:T(8,128)}, f32[256,256]{1,0:T(8,128)}, f32[256,256]{1,0:T(8,128)}, f32[256,128]{1,0:T(8,128)}, f32[128,256]{1,0:T(8,128)}, /*index=5*/f32[256,256]{1,0:T(8,128)}) custom-call(f32[256,256]{1,0:T(8,128)S(1)} %get-tuple-element.12.refs_0_, f32[256,256]{1,0:T(8,128)S(1)} %get-tuple-element.13.refs_1_, ...), custom_call_target="tpu_custom_call" | custom-call | tf_op jit(solution)/shard_map/pallas_call | solution.py:474

commit v3 on v2

v3 whole, which is shorter than its diff:
```python
import functools

import jax
import jax.numpy as jnp
from jax import lax
from jax.experimental import pallas as pl
from jax.experimental.pallas import tpu as pltpu
from jax.sharding import PartitionSpec as P

MESH = pl.DeviceIdType.MESH
F32 = jnp.float32
BF16 = jnp.bfloat16
NC = 16
NA = 32
NZ = 16
ALPHA = 0.25 / 12.0
CH = 32
CHS = 128
CHF = 64
PLANE = sorted(
    ((dy, dx, dc) for dy in range(4) for dx in range(4) for dc in range(2) if (dy, dx, dc) != (0, 0, 0)),
    key=lambda d: -(min(d[0], 4 - d[0]) + min(d[1], 4 - d[1])),
)


def split(x):
    hi = x.astype(BF16)
    return hi, (x - hi.astype(F32)).astype(BF16)


def dot3(a, b):
    dot = functools.partial(jnp.dot, preferred_element_type=F32)
    (ah, al), (bh, bl) = a, b
    return dot(ah, bh) + (dot(ah, bl) + dot(al, bh))


def d12(f, axis):
    n = f.shape[axis]
    up1, dn1 = pltpu.roll(f, n - 1, axis), pltpu.roll(f, 1, axis)
    up2, dn2 = pltpu.roll(f, n - 2, axis), pltpu.roll(f, 2, axis)
    return 8.0 * (up1 - dn1) - (up2 - dn2)


def kernel(
    e_in, p_in, q_in, c_in, w_in, om_in, th_in, l_in, r_in,
    sv, pv, qv, rsum, csum, zsum,
    fld, wid, hal, haw, tsl, asl, bsl, xs, xb, sph, wpx, e1x, wcs, frs, zx, zy, edg, shl,
    om, th, lm, rm, omh, thh, lmh, rmh,
    rpart, cpart, kpart, rrec, crec, krec, zrec, ksum,
    in_sem, row_s, row_r, col_s, col_r, cor_s, cor_r,
    rs_s, rs_r, ag_s, ag_r, near,
):
    cross = lax.axis_index("cross")
    along = lax.axis_index("along")
    z, ylo = along // 2, along % 2
    yhi, x_at, core = cross // 8, cross // 2 % 4, cross % 2
    y_at = yhi * 2 + ylo
    plane = y_at * 8 + x_at * 2 + core

    loads = [
        pltpu.make_async_copy(src, fld.at[k, pl.ds(8, 256)], in_sem.at[k])
        for k, src in enumerate((e_in, p_in, q_in, c_in))
    ]
    loads.append(pltpu.make_async_copy(w_in, wid.at[pl.ds(8, 256)], in_sem.at[4]))
    for copy in loads:
        copy.start()
    mats = [
        pltpu.make_async_copy(src, dst, in_sem.at[5 + k])
        for k, (src, dst) in enumerate(((om_in, om), (th_in, th), (l_in, lm), (r_in, rm)))
    ]
    for copy in mats:
        copy.start()

    rem = lax.rem

    def along_peer(d):
        return {"cross": cross, "along": rem(along + d, NA)}

    def cross_peer(d):
        return {"cross": rem(cross + d, NC), "along": along}

    def plane_at(dy, dx, dc):
        return rem(y_at + dy, 4), rem(x_at + dx, 4), rem(core + dc, 2)

    def plane_peer(dy, dx, dc):
        y, x, c = plane_at(dy, dx, dc)
        return {"cross": lax.div(y, 2) * 8 + x * 2 + c, "along": z * 2 + rem(y, 2)}

    def z_peer(d, y=ylo):
        return {"cross": cross, "along": rem(z + d, NZ) * 2 + y}

    def signal(sem, peer):
        pl.semaphore_signal(sem, inc=1, device_id=peer, device_id_type=MESH)

    barrier = pltpu.get_barrier_semaphore()
    for d in (1, NZ - 1):
        for y in range(2):
            signal(barrier, z_peer(d, y))

    for d in PLANE:
        signal(barrier, plane_peer(*d))

    def tell(k):
        for d in (2**k, NZ - 2**k):
            signal(near.at[k], z_peer(d))

    def hear(k):
        pl.semaphore_wait(near.at[k], 2)

    for copy in loads:
        copy.wait()

    lane = lax.broadcasted_iota(jnp.int32, (128, 128), 1)
    for b in range(2):
        rows = pl.ds(8 + 128 * b, 128)
        fields = [wid[rows].astype(F32)] + [fld[k, rows] for k in (1, 2, 0, 3)]
        slab = jnp.zeros((128, 128), F32)
        for k, f in enumerate(fields):
            x = pltpu.roll(jnp.where(lane < 64, f[:, :128], f[:, 128:]), 8 * (k + 1), 1)
            slab = jnp.where((lane >= 8 * k + 4) & (lane < 8 * k + 12), x, slab)
        tsl[:, :, pl.ds(128 * b, 128)] = slab.T.reshape(16, 8, 128)

    @pl.when(along == 0)
    def _():
        asl[7:11, 4:8] = jnp.zeros((4, 4, 256), F32)
        asl[11, 4:8] = jnp.ones((4, 256), F32)

    @pl.when(along == NA - 1)
    def _():
        asl[0:4, 0:4] = jnp.zeros((4, 4, 256), F32)
        asl[4, 0:4] = jnp.ones((4, 256), F32)

    for side, edge in enumerate((0, NC - 1)):

        @pl.when(cross == edge)
        def _():
            hal[0:3, side] = jnp.zeros((3, 8, 256), F32)
            hal[3, side] = jnp.ones((8, 256), F32)
            haw[side] = jnp.zeros((8, 256), jnp.int32)
            bsl[side] = jnp.zeros((16, 8, 128), F32)

    pl.semaphore_wait(barrier, NA - 1 + 4)
    tell(0)

    def remote(src, dst, sems, k, peer):
        return pltpu.make_async_remote_copy(
            src_ref=src,
            dst_ref=dst,
            send_sem=sems[0].at[k],
            recv_sem=sems[1].at[k],
            device_id=peer,
            device_id_type=MESH,
        )

    cols = [
        remote(tsl.at[pl.ds(0, 5), pl.ds(4, 4)], asl.at[pl.ds(7, 5), pl.ds(4, 4)], (col_s, col_r), 0, along_peer(1)),
        remote(tsl.at[pl.ds(1, 5), pl.ds(0, 4)], asl.at[pl.ds(0, 5), pl.ds(0, 4)], (col_s, col_r), 1, along_peer(NA - 1)),
    ]
    halo = [[], []]
    for side, (src, dst, step) in enumerate(((260, 4, 1), (8, 0, NC - 1))):
        for k in (0, 1, 4, 3, 2):
            ref, to = (wid, haw) if k == 4 else (fld.at[k], hal.at[k])
            halo[side].append(
                remote(
                    ref.at[pl.ds(src, 4)], to.at[side, pl.ds(dst, 4)], (row_s, row_r), 2 * k + side, cross_peer(step)
                )
            )
    goes = (cross < NC - 1, cross > 0)
    comes = (cross > 0, cross < NC - 1)
    goes_a = (along < NA - 1, along > 0)
    comes_a = (along > 0, along < NA - 1)

    def only(cond, *acts):
        @pl.when(cond)
        def _():
            for act in acts:
                act()

    for side in range(2):
        only(goes[side], *[copy.start for copy in halo[side]])
    for side in range(2):
        only(goes_a[side], cols[side].start)

    for copy in mats:
        copy.wait()
    for src, dst in ((om, omh), (th, thh), (lm, lmh), (rm, rmh)):
        hi, lo = split(src[...])
        dst[0] = hi
        dst[1] = lo

    def coefficients(w, c):
        return w * c * ALPHA, w * (0.02 / c)

    zero8 = jnp.zeros((8, 256), F32)
    for ref in (fld.at[0], sph):
        ref[pl.ds(0, 8)] = zero8
        ref[pl.ds(264, 8)] = zero8


    def edges(f):
        lanes = lax.broadcasted_iota(jnp.int32, (CH, 128), 1)
        return jnp.where(lanes >= 96, f[:, 128:], pltpu.roll(f[:, :128], 64, 1))

    def inside(i):
        r0 = pl.multiple_of(i * CH, 8)
        here = pl.ds(r0, CH)
        own = pl.ds(pl.multiple_of(8 + i * CH, 8), CH)
        w = wid[own].astype(F32)
        e, p, q, c = (fld[k, own] for k in range(4))
        wc, fr = coefficients(w, c)
        wcs[here] = wc
        frs[here] = fr
        wp, wq = w * p, w * q
        wpx[own] = wp
        de = d12(fld[0, pl.ds(r0, CH + 16)], 0)[8 : 8 + CH]
        sph[own] = 2.0 * wp - wc * de - fr * wp
        sq = 2.0 * wq - wc * d12(e, 1) - fr * wq
        zy[here] = d12(sq, 1)
        for k, f in enumerate((w, wq, e, wc, fr)):
            edg[k, here] = edges(f)

    pl.loop(0, 128 // CH)(inside)
    hear(0)
    tell(1)
    pl.loop(128 // CH, 256 // CH)(inside)

    @pl.loop(0, 256 // CH)
    def _(i):
        r0 = pl.multiple_of(i * CH, 8)
        zx[pl.ds(r0, CH)] = d12(sph[pl.ds(r0, CH + 16)], 0)[8 : 8 + CH]

    for side in range(2):
        only(comes_a[side], cols[side].wait_recv)
    hear(1)
    tell(2)

    corners = []
    for side, step in enumerate((1, NC - 1)):
        part = pl.ds(128 * (1 - side), 128)
        corners.append(
            [
                remote(
                    asl.at[pl.ds(tile, 3), pl.ds(row, 4), part],
                    bsl.at[side, pl.ds(tile, 3), pl.ds(row, 4)],
                    (cor_s, cor_r),
                    2 * side + k,
                    cross_peer(step),
                )
                for k, (tile, row) in enumerate(((0, 0), (7, 4)))
            ]
        )
    for side in range(2):
        only(goes[side], *[copy.start for copy in corners[side]])

    for b in range(2):
        xs[pl.ds(128 * b, 128)] = asl[:, :, pl.ds(128 * b, 128)].reshape(128, 128).T

    def beside(x, k):
        return pltpu.roll(x, 128 - 8 * k, 1) if k else x

    for side in range(2):
        only(comes[side], *[copy.wait_recv for copy in halo[side]])
    for side, at in enumerate((0, 264)):
        for k in range(4):
            fld[k, pl.ds(at, 8)] = hal[k, side]
        wid[pl.ds(at, 8)] = haw[side]

    for at, off in ((0, 0), (256, 8)):
        rows = pl.ds(at, 16)
        w = wid[rows].astype(F32)
        wc, fr = coefficients(w, fld[3, rows])
        wp = w * fld[1, rows]
        wpx[rows] = wp
        de = d12(fld[0, pl.ds(at - off, 24)], 0)[off : off + 16]
        sph[rows] = 2.0 * wp - wc * de - fr * wp
    zx[pl.ds(0, 8)] = d12(sph[pl.ds(0, 24)], 0)[8:16]
    zx[pl.ds(248, 8)] = d12(sph[pl.ds(248, 24)], 0)[8:16]

    @pl.loop(0, 256 // CHS)
    def _(i):
        here = pl.ds(pl.multiple_of(i * CHS, 8), CHS)
        own = pl.ds(pl.multiple_of(8 + i * CHS, 8), CHS)
        x = xs[here]
        lanes = lax.broadcasted_iota(jnp.int32, (CHS, 128), 1)
        w = beside(x, 0)
        wc, fr = coefficients(w, beside(x, 4))
        w, wq, e, wc, fr = (
            jnp.where(lanes < 64, new, edg[k, here])
            for k, new in enumerate((w, w * beside(x, 2), beside(x, 3), wc, fr))
        )
        dy = d12(2.0 * wq - wc * d12(e, 1) - fr * wq, 1)
        z_y = zy[here]
        z_y = jnp.concatenate(
            [
                jnp.where(lanes < 8, pltpu.roll(dy, 64, 1), z_y[:, :128]),
                jnp.where(lanes >= 120, dy, z_y[:, 128:]),
            ],
            axis=1,
        )
        en = fld[0, own] - (0.5 * ALPHA) * wid[own].astype(F32) * (zx[here] + z_y)
        sv[here] = en
        hi, lo = split(en)
        shl[0, here] = hi
        shl[1, here] = lo

    def send(n, peer, src, dst, phase, s_sem, r_sem):
        def one(d):
            pltpu.make_async_remote_copy(
                src_ref=src(d),
                dst_ref=dst(d),
                send_sem=s_sem.at[phase],
                recv_sem=r_sem.at[phase],
                device_id=peer(*d) if peer is plane_peer else peer(d),
                device_id_type=MESH,
            ).start()

        if peer is plane_peer:
            for d in PLANE:
                one(d)
            return
        one(n // 2)

        @pl.loop(1, n // 2)
        def _(s):
            one(n // 2 - s)
            one(n // 2 + s)

    def await_recv(ref, sem):
        pltpu.make_async_copy(ref, ref, sem).wait()

    def place(y, x, c):
        return y * 8 + x * 2 + c

    surf = (shl[0], shl[1])
    tr = dot3(surf, (rmh[0], rmh[1]))
    kpart[...] = dot3((lmh[0], lmh[1]), split(tr)).reshape(NA, 8, 256)
    send(NA, plane_peer, lambda d: kpart.at[place(*plane_at(*d))], lambda d: krec.at[place(*d)], 1, rs_s, rs_r)
    rpart[...] = dot3(surf, (omh[0], omh[1])).reshape(NA, 8, 128)
    cpart[...] = dot3((thh[0], thh[1]), surf).reshape(NC, 8, 256)
    hear(2)
    send(NA, along_peer, lambda d: rpart.at[rem(along + d, NA)], lambda d: rrec.at[d], 0, rs_s, rs_r)

    for side in range(2):
        only(comes[side], *[copy.wait_recv for copy in corners[side]])
    for side in range(2):
        t = bsl[side].reshape(128, 128).T
        xb[pl.ds(8 * side, 8)] = t[120:128] if side == 0 else t[0:8]

    def ring(x):
        lane = lax.broadcasted_iota(jnp.int32, x.shape, 1)
        return jnp.where(lane < 32, x, pltpu.roll(x, 64, 1))

    def e1_rows(r, n, x, lead):
        w = wid[pl.ds(r, n)].astype(F32)
        wq = jnp.concatenate([w * fld[2, pl.ds(r, n)], ring(beside(x, 0) * beside(x, 2))], axis=1)
        wp = wpx[pl.ds(pl.multiple_of(r - lead, 8), n + 16)]
        dx = d12(wp, 0)[lead : lead + n]
        dy = d12(wq, 1)[:, :256]
        e = fld[0, pl.ds(r, n)]
        return e + (e - ALPHA * w * (dx + dy))

    @pl.loop(0, 256 // CHF)
    def _(i):
        r = pl.multiple_of(8 + i * CHF, 8)
        e1x[pl.ds(r, CHF)] = e1_rows(r, CHF, xs[pl.ds(pl.multiple_of(i * CHF, 8), CHF)], 8)

    e1x[pl.ds(0, 8)] = e1_rows(0, 8, xb[pl.ds(0, 8)], 0)
    e1x[pl.ds(264, 8)] = e1_rows(264, 8, xb[pl.ds(8, 8)], 16)

    send(NC, cross_peer, lambda d: cpart.at[rem(cross + d, NC)], lambda d: crec.at[d], 2, rs_s, rs_r)

    await_recv(krec.at[pl.ds(1, NA - 1)], rs_r.at[1])
    krec[0] = kpart[plane]
    ksum[...] = jnp.sum(krec[...], axis=0)
    send(NZ, z_peer, lambda d: ksum, lambda d: zrec.at[d], 3, rs_s, rs_r)

    xb[pl.ds(16, 256)] = xs[...]

    @pl.loop(0, 256 // CHF)
    def _(i):
        r0 = pl.multiple_of(i * CHF, 8)
        r = pl.multiple_of(8 + i * CHF, 8)
        own = pl.ds(r, CHF)
        x = xs[pl.ds(r0, CHF)]
        w = wid[own].astype(F32)
        p, q = fld[1, own], fld[2, own]
        wc, fr = wcs[pl.ds(r0, CHF)], frs[pl.ds(r0, CHF)]
        p1 = p - wc * d12(fld[0, pl.ds(r0, CHF + 16)], 0)[8 : 8 + CHF] - fr * p
        ee = e1x[pl.ds(r0, CHF + 16)]
        dx = d12(ee, 0)[8 : 8 + CHF]
        pv[pl.ds(r0, CHF)] = p - 0.5 * (wc * dx + fr * (p + p1))

        hb = jnp.concatenate(
            [
                jnp.where(i == 0, xb[pl.ds(0, 8)], xb[pl.ds(pl.multiple_of(jnp.maximum(r0 + 8, 8), 8), 8)]),
                x,
                jnp.where(
                    i == 256 // CHF - 1,
                    xb[pl.ds(8, 8)],
                    xb[pl.ds(pl.multiple_of(jnp.minimum(r0 + 16 + CHF, 264), 8), 8)],
                ),
            ],
            axis=0,
        )
        wpb = ring(beside(hb, 0) * beside(hb, 1))
        dxb = d12(wpb, 0)[8 : 8 + CHF]
        wb = ring(beside(x, 0))
        wq = jnp.concatenate([w * q, ring(beside(x, 0) * beside(x, 2))], axis=1)
        dyb = d12(wq, 1)[:, 256:]
        eb = ring(beside(x, 3))
        e1b = eb + (eb - ALPHA * wb * (dxb + dyb))
        e = jnp.concatenate([fld[0, own], eb], axis=1)
        q1 = q - wc * d12(e, 1)[:, :256] - fr * q
        dy = d12(jnp.concatenate([e1x[own], e1b], axis=1), 1)[:, :256]
        qv[pl.ds(r0, CHF)] = q - 0.5 * (wc * dy + fr * (q + q1))

    await_recv(rrec.at[pl.ds(1, NA - 1)], rs_r.at[0])
    rrec[0] = rpart[along]
    rsum[z, ylo] = jnp.sum(rrec[...], axis=0)
    own_r = rsum.at[z, ylo]
    send(NZ, z_peer, lambda d: own_r, lambda d: own_r, 0, ag_s, ag_r)

    await_recv(crec.at[pl.ds(1, NC - 1)], rs_r.at[2])
    crec[0] = cpart[cross]
    csum[pl.ds(pl.multiple_of(8 * cross, 8), 8)] = jnp.sum(crec[...], axis=0)
    mine = pl.ds(pl.multiple_of(8 * cross, 8), 8)
    send(NC, cross_peer, lambda d: csum.at[mine], lambda d: csum.at[mine], 2, ag_s, ag_r)

    await_recv(zrec.at[pl.ds(1, NZ - 1)], rs_r.at[3])
    zrec[0] = ksum[...]
    total = zrec[z]
    for k in range(1, NZ):
        total = total + zrec[rem(z - k + NZ, NZ)]
    own_k = pl.ds(pl.multiple_of(8 * plane, 8), 8)
    zsum[own_k] = total
    send(NA, plane_peer, lambda d: zsum.at[own_k], lambda d: zsum.at[own_k], 1, ag_s, ag_r)

    await_recv(csum.at[pl.ds(0, 120)], ag_r.at[2])
    await_recv(rsum.at[pl.ds(0, NZ - 1), 0], ag_r.at[0])
    pair = pltpu.make_async_remote_copy(
        src_ref=rsum.at[:, ylo],
        dst_ref=rsum.at[:, ylo],
        send_sem=ag_s.at[3],
        recv_sem=ag_r.at[3],
        device_id={"cross": cross, "along": z * 2 + 1 - ylo},
        device_id_type=MESH,
    )
    pair.start()
    await_recv(zsum.at[pl.ds(0, 248)], ag_r.at[1])
    pair.wait_recv()

    for side in range(2):
        only(goes[side], *[copy.wait_send for copy in halo[side] + corners[side]])
        only(goes_a[side], cols[side].wait_send)
    pair.wait_send()
    await_recv(rrec.at[pl.ds(1, NA - 1)], rs_s.at[0])
    await_recv(krec.at[pl.ds(1, NA - 1)], rs_s.at[1])
    await_recv(crec.at[pl.ds(1, NC - 1)], rs_s.at[2])
    await_recv(zrec.at[pl.ds(1, NZ - 1)], rs_s.at[3])
    await_recv(rsum.at[pl.ds(0, NZ - 1), 0], ag_s.at[0])
    await_recv(zsum.at[pl.ds(0, 248)], ag_s.at[1])
    await_recv(csum.at[pl.ds(0, 120)], ag_s.at[2])


def write_out(*refs):
    ins, outs, sem = refs[:6], refs[6:12], refs[12]
    copies = [pltpu.make_async_copy(a, b, sem.at[k]) for k, (a, b) in enumerate(zip(ins, outs))]
    for copy in copies:
        copy.start()
    for copy in copies:
        copy.wait()


def body(*args):
    vm = pltpu.VMEM
    dma = pltpu.SemaphoreType.DMA
    sds = jax.ShapeDtypeStruct
    held = pl.pallas_call(
        kernel,
        out_shape=(
            sds((256, 256), F32),
            sds((256, 256), F32),
            sds((256, 256), F32),
            sds((NZ, 2, 8, 128), F32),
            sds((128, 256), F32),
            sds((256, 256), F32),
        ),
        in_specs=[pl.BlockSpec(memory_space=pl.ANY)] * 9,
        out_specs=[pl.BlockSpec(memory_space=pltpu.VMEM)] * 6,
        scratch_shapes=[
            vm((4, 272, 256), F32),
            vm((272, 256), jnp.int32),
            vm((4, 2, 8, 256), F32),
            vm((2, 8, 256), jnp.int32),
            vm((16, 8, 256), F32),
            vm((16, 8, 256), F32),
            vm((2, 16, 8, 128), F32),
            vm((256, 128), F32),
            vm((272, 128), F32),
            vm((272, 256), F32),
            vm((272, 256), F32),
            vm((272, 256), F32),
            vm((256, 256), F32),
            vm((256, 256), F32),
            vm((256, 256), F32),
            vm((256, 256), F32),
            vm((5, 256, 128), F32),
            vm((2, 256, 256), BF16),
            vm((256, 128), F32),
            vm((128, 256), F32),
            vm((256, 256), F32),
            vm((256, 256), F32),
            vm((2, 256, 128), BF16),
            vm((2, 128, 256), BF16),
            vm((2, 256, 256), BF16),
            vm((2, 256, 256), BF16),
            vm((NA, 8, 128), F32),
            vm((NC, 8, 256), F32),
            vm((NA, 8, 256), F32),
            vm((NA, 8, 128), F32),
            vm((NC, 8, 256), F32),
            vm((NA, 8, 256), F32),
            vm((NZ, 8, 256), F32),
            vm((8, 256), F32),
            dma((9,)),
            dma((10,)),
            dma((10,)),
            dma((2,)),
            dma((2,)),
            dma((4,)),
            dma((4,)),
            dma((4,)),
            dma((4,)),
            dma((4,)),
            dma((4,)),
            pltpu.SemaphoreType.REGULAR((3,)),
        ],
        compiler_params=pltpu.CompilerParams(collective_id=0, has_side_effects=True, vmem_limit_bytes=16 << 20),
    )(*[pltpu.with_memory_space_constraint(a, pltpu.HBM) for a in args])
    held = held[:3] + (held[3].reshape(256, 128),) + held[4:]
    return pl.pallas_call(
        write_out,
        out_shape=tuple(sds(x.shape, F32) for x in held),
        in_specs=[pl.BlockSpec(memory_space=pltpu.VMEM)] * 6,
        out_specs=[pl.BlockSpec(memory_space=pl.ANY)] * 6,
        scratch_shapes=[dma((6,))],
        compiler_params=pltpu.CompilerParams(vmem_limit_bytes=8 << 20),
    )(*held)


def solution(mesh):
    return jax.shard_map(
        body,
        mesh=mesh,
        in_specs=(
            P("cross", "along"),
            P("cross", "along"),
            P("cross", "along"),
            P("cross", "along"),
            P("cross", "along"),
            P("along", None),
            P(None, "cross"),
            P(None, "cross"),
            P("along", None),
        ),
        out_specs=(
            P("cross", "along"),
            P("cross", "along"),
            P("cross", "along"),
            P("cross", None),
            P(None, "along"),
            P(),
        ),
        check_vma=False,
    )
```

time: 48.5 us -> 43.9 us (0.905)
  Pallas kernels: 47.8 us -> 43.1 us
    pallas_call x1, Pallas kernels: 46.7 us -> 42 us  [body(): pl.pallas_call(kernel, out_shape=(sds((256, 256), F32), sds((256, 256), F...]
where the time goes in v3:
time: 43.9 us; the launch traced here: 43.7 us
  Pallas kernels  43.1 us (98%)
  between operations  0.64 us (1%)
    pallas_call x1, Pallas kernels, body(): pl.pallas_call(kernel, out_shape=(sds((256, 256), F32), sds((256, 256), F...  42 us
    pallas_call x1, Pallas kernels, body(): pl.pallas_call(write_out, out_shape=tuple((sds(x.shape, F32) for x in hel...  1.1 us

profile of v3, /device:TPU:1, one launch (start us, length us, event | category | flops | bytes accessed | tf_op | source)
XLA Modules:
  0.0 43.7 jit_solution(111106361609174635)
XLA Ops:
  0.6 42.0 %shard_map.136 = (f32[256,256]{1,0:T(8,128)S(1)}, f32[256,256]{1,0:T(8,128)S(1)}, f32[256,256]{1,0:T(8,128)S(1)}, f32[16,2,8,128]{3,2,1,0:T(8,128)S(1)}, f32[128,256]{1,0:T(8,128)S(1)}, /*index=5*/f32[256,256]{1,0:T(8,128)S(1)}) custom-call(f32[256,256]{1,0:T(8,128)} %e_in.1, f32[256,256]{1,0:T(8,128)} %p_in.1, f32[256,256]{1,0:T(8,128)} %q_in.1, ...), custom_call_target="tpu_custom_call" | custom-call | tf_op jit(solution)/shard_map/pallas_call | solution.py:478
  42.6 1.1 %shard_map.137 = (f32[256,256]{1,0:T(8,128)}, f32[256,256]{1,0:T(8,128)}, f32[256,256]{1,0:T(8,128)}, f32[256,128]{1,0:T(8,128)}, f32[128,256]{1,0:T(8,128)}, /*index=5*/f32[256,256]{1,0:T(8,128)}) custom-call(f32[256,256]{1,0:T(8,128)S(1)} %get-tuple-element.12.refs_0_, f32[256,256]{1,0:T(8,128)S(1)} %get-tuple-element.13.refs_1_, ...), custom_call_target="tpu_custom_call" | custom-call | tf_op jit(solution)/shard_map/pallas_call | solution.py:541

commit v4 on v3

--- a/solution.py
+++ b/solution.py
@@ -14,13 +14,15 @@
 NA = 32
 NZ = 16
 ALPHA = 0.25 / 12.0
-CH = 32
-CHS = 128
+CH = 64
+CHS = 256
 CHF = 64
 PLANE = sorted(
     ((dy, dx, dc) for dy in range(4) for dx in range(4) for dc in range(2) if (dy, dx, dc) != (0, 0, 0)),
     key=lambda d: -(min(d[0], 4 - d[0]) + min(d[1], 4 - d[1])),
 )
+
+NEXT = [d for d in PLANE if min(d[0], 4 - d[0]) + min(d[1], 4 - d[1]) <= 2]
 
 
 def split(x):
@@ -93,19 +95,33 @@
         pl.semaphore_signal(sem, inc=1, device_id=peer, device_id_type=MESH)
 
     barrier = pltpu.get_barrier_semaphore()
-    for d in (1, NZ - 1):
+    first, last = cross == 0, cross == NC - 1
+
+    @pl.when(jnp.logical_not(first))
+    def _():
+        signal(barrier, cross_peer(NC - 1))
+
+    @pl.when(jnp.logical_not(last))
+    def _():
+        signal(barrier, cross_peer(1))
+
+    for d in (2, NZ - 2, 1, NZ - 1):
         for y in range(2):
             signal(barrier, z_peer(d, y))
-
-    for d in PLANE:
+    for d in NEXT:
         signal(barrier, plane_peer(*d))
 
     def tell(k):
-        for d in (2**k, NZ - 2**k):
+        for d in (2 << k, NZ - (2 << k)):
             signal(near.at[k], z_peer(d))
+        if k == 0:
+            for d in ((0, 2, 0), (2, 0, 0)):
+                signal(near.at[2], plane_peer(*d))
 
     def hear(k):
         pl.semaphore_wait(near.at[k], 2)
+        if k == 0:
+            pl.semaphore_wait(near.at[2], 2)
 
     for copy in loads:
         copy.wait()
@@ -139,7 +155,7 @@
             haw[side] = jnp.zeros((8, 256), jnp.int32)
             bsl[side] = jnp.zeros((16, 8, 128), F32)
 
-    pl.semaphore_wait(barrier, NA - 1 + 4)
+    pl.semaphore_wait(barrier, len(NEXT) + 10 - jnp.where(first, 1, 0) - jnp.where(last, 1, 0))
     tell(0)
 
     def remote(src, dst, sems, k, peer):
@@ -219,20 +235,17 @@
         for k, f in enumerate((w, wq, e, wc, fr)):
             edg[k, here] = edges(f)
 
-    pl.loop(0, 128 // CH)(inside)
-    hear(0)
-    tell(1)
-    pl.loop(128 // CH, 256 // CH)(inside)
+    pl.loop(0, 256 // CH)(inside)
 
     @pl.loop(0, 256 // CH)
     def _(i):
         r0 = pl.multiple_of(i * CH, 8)
         zx[pl.ds(r0, CH)] = d12(sph[pl.ds(r0, CH + 16)], 0)[8 : 8 + CH]
 
+    hear(0)
+    tell(1)
     for side in range(2):
         only(comes_a[side], cols[side].wait_recv)
-    hear(1)
-    tell(2)
 
     corners = []
     for side, step in enumerate((1, NC - 1)):
@@ -337,7 +350,7 @@
     send(NA, plane_peer, lambda d: kpart.at[place(*plane_at(*d))], lambda d: krec.at[place(*d)], 1, rs_s, rs_r)
     rpart[...] = dot3(surf, (omh[0], omh[1])).reshape(NA, 8, 128)
     cpart[...] = dot3((thh[0], thh[1]), surf).reshape(NC, 8, 256)
-    hear(2)
+    hear(1)
     send(NA, along_peer, lambda d: rpart.at[rem(along + d, NA)], lambda d: rrec.at[d], 0, rs_s, rs_r)
 
     for side in range(2):
@@ -418,7 +431,32 @@
     rrec[0] = rpart[along]
     rsum[z, ylo] = jnp.sum(rrec[...], axis=0)
     own_r = rsum.at[z, ylo]
-    send(NZ, z_peer, lambda d: own_r, lambda d: own_r, 0, ag_s, ag_r)
+
+    def on_z(d, k):
+        pltpu.make_async_remote_copy(
+            src_ref=own_r,
+            dst_ref=own_r,
+            send_sem=ag_s.at[0],
+            recv_sem=ag_r.at[k],
+            device_id=z_peer(d),
+            device_id_type=MESH,
+        ).start()
+
+    for d in (8, 7, 9, 6, 10, 5, 11):
+        on_z(d, 0)
+    for d in (4, 12, 3, 13, 2, 14, 1, 15):
+        on_z(d, 4)
+
+    def to_pair(d):
+        there = rsum.at[rem(z + d, NZ), ylo]
+        pltpu.make_async_remote_copy(
+            src_ref=there,
+            dst_ref=there,
+            send_sem=ag_s.at[3],
+            recv_sem=ag_r.at[3],
+            device_id={"cross": cross, "along": z * 2 + 1 - ylo},
+            device_id_type=MESH,
+        ).start()
 
     await_recv(crec.at[pl.ds(1, NC - 1)], rs_r.at[2])
     crec[0] = cpart[cross]
@@ -435,24 +473,21 @@
     zsum[own_k] = total
     send(NA, plane_peer, lambda d: zsum.at[own_k], lambda d: zsum.at[own_k], 1, ag_s, ag_r)
 
+    await_recv(rsum.at[pl.ds(0, 8), 0], ag_r.at[4])
+    for d in (0, 1, 15, 2, 14, 3, 13, 4, 12):
+        to_pair(d)
+
     await_recv(csum.at[pl.ds(0, 120)], ag_r.at[2])
-    await_recv(rsum.at[pl.ds(0, NZ - 1), 0], ag_r.at[0])
-    pair = pltpu.make_async_remote_copy(
-        src_ref=rsum.at[:, ylo],
-        dst_ref=rsum.at[:, ylo],
-        send_sem=ag_s.at[3],
-        recv_sem=ag_r.at[3],
-        device_id={"cross": cross, "along": z * 2 + 1 - ylo},
-        device_id_type=MESH,
-    )
-    pair.start()
+    await_recv(rsum.at[pl.ds(0, 7), 0], ag_r.at[0])
+    for d in (5, 11, 6, 10, 7, 9, 8):
+        to_pair(d)
     await_recv(zsum.at[pl.ds(0, 248)], ag_r.at[1])
-    pair.wait_recv()
+    await_recv(rsum.at[:, 0], ag_r.at[3])
 
     for side in range(2):
         only(goes[side], *[copy.wait_send for copy in halo[side] + corners[side]])
         only(goes_a[side], cols[side].wait_send)
-    pair.wait_send()
+    await_recv(rsum.at[:, 0], ag_s.at[3])
     await_recv(rrec.at[pl.ds(1, NA - 1)], rs_s.at[0])
     await_recv(krec.at[pl.ds(1, NA - 1)], rs_s.at[1])
     await_recv(crec.at[pl.ds(1, NC - 1)], rs_s.at[2])
@@ -532,7 +567,7 @@
             dma((4,)),
             dma((4,)),
             dma((4,)),
-            dma((4,)),
+            dma((5,)),
             pltpu.SemaphoreType.REGULAR((3,)),
         ],
         compiler_params=pltpu.CompilerParams(collective_id=0, has_side_effects=True, vmem_limit_bytes=16 << 20),

time: 43.9 us -> 42.6 us (0.970)
  Pallas kernels: 43.1 us -> 41.8 us
    pallas_call x1, Pallas kernels: 42 us -> 40.7 us  [body(): pl.pallas_call(kernel, out_shape=(sds((256, 256), F32), sds((256, 256), F...]
where the time goes in v4:
time: 42.6 us; the launch traced here: 42.5 us
  Pallas kernels  41.8 us (98%)
  between operations  0.64 us (2%)
    pallas_call x1, Pallas kernels, body(): pl.pallas_call(kernel, out_shape=(sds((256, 256), F32), sds((256, 256), F...  40.7 us
    pallas_call x1, Pallas kernels, body(): pl.pallas_call(write_out, out_shape=tuple((sds(x.shape, F32) for x in hel...  1.1 us

profile of v4, /device:TPU:1, one launch (start us, length us, event | category | flops | bytes accessed | tf_op | source)
XLA Modules:
  0.0 42.5 jit_solution(9212215196830709642)
XLA Ops:
  0.6 40.7 %shard_map.136 = (f32[256,256]{1,0:T(8,128)S(1)}, f32[256,256]{1,0:T(8,128)S(1)}, f32[256,256]{1,0:T(8,128)S(1)}, f32[16,2,8,128]{3,2,1,0:T(8,128)S(1)}, f32[128,256]{1,0:T(8,128)S(1)}, /*index=5*/f32[256,256]{1,0:T(8,128)S(1)}) custom-call(f32[256,256]{1,0:T(8,128)} %e_in.1, f32[256,256]{1,0:T(8,128)} %p_in.1, f32[256,256]{1,0:T(8,128)} %q_in.1, ...), custom_call_target="tpu_custom_call" | custom-call | tf_op jit(solution)/shard_map/pallas_call | solution.py:513
  41.4 1.1 %shard_map.137 = (f32[256,256]{1,0:T(8,128)}, f32[256,256]{1,0:T(8,128)}, f32[256,256]{1,0:T(8,128)}, f32[256,128]{1,0:T(8,128)}, f32[128,256]{1,0:T(8,128)}, /*index=5*/f32[256,256]{1,0:T(8,128)}) custom-call(f32[256,256]{1,0:T(8,128)S(1)} %get-tuple-element.12.refs_0_, f32[256,256]{1,0:T(8,128)S(1)} %get-tuple-element.13.refs_1_, ...), custom_call_target="tpu_custom_call" | custom-call | tf_op jit(solution)/shard_map/pallas_call | solution.py:576

commit v5 on v4

--- a/solution.py
+++ b/solution.py
@@ -385,7 +385,12 @@
     await_recv(krec.at[pl.ds(1, NA - 1)], rs_r.at[1])
     krec[0] = kpart[plane]
     ksum[...] = jnp.sum(krec[...], axis=0)
-    send(NZ, z_peer, lambda d: ksum, lambda d: zrec.at[d], 3, rs_s, rs_r)
+
+    @pl.loop(0, NZ - 1)
+    def _(k):
+        d = rem(k + jnp.where(k >= z, 1, 0) - z + NZ, NZ)
+        remote(ksum, zrec.at[d], (rs_s, rs_r), 3, z_peer(d)).start()
+
 
     xb[pl.ds(16, 256)] = xs[...]
 

time: 42.6 us -> 41.7 us (0.979)
  Pallas kernels: 41.8 us -> 40.9 us
    pallas_call x1, Pallas kernels: 40.7 us -> 39.8 us  [body(): pl.pallas_call(kernel, out_shape=(sds((256, 256), F32), sds((256, 256), F...]
where the time goes in v5:
time: 41.7 us; the launch traced here: 41.5 us
  Pallas kernels  40.9 us (98%)
  between operations  0.64 us (2%)
    pallas_call x1, Pallas kernels, body(): pl.pallas_call(kernel, out_shape=(sds((256, 256), F32), sds((256, 256), F...  39.8 us
    pallas_call x1, Pallas kernels, body(): pl.pallas_call(write_out, out_shape=tuple((sds(x.shape, F32) for x in hel...  1.1 us

profile of v5, /device:TPU:1, one launch (start us, length us, event | category | flops | bytes accessed | tf_op | source)
XLA Modules:
  0.0 41.5 jit_solution(9624151286369890752)
XLA Ops:
  0.6 39.8 %shard_map.136 = (f32[256,256]{1,0:T(8,128)S(1)}, f32[256,256]{1,0:T(8,128)S(1)}, f32[256,256]{1,0:T(8,128)S(1)}, f32[16,2,8,128]{3,2,1,0:T(8,128)S(1)}, f32[128,256]{1,0:T(8,128)S(1)}, /*index=5*/f32[256,256]{1,0:T(8,128)S(1)}) custom-call(f32[256,256]{1,0:T(8,128)} %e_in.1, f32[256,256]{1,0:T(8,128)} %p_in.1, f32[256,256]{1,0:T(8,128)} %q_in.1, ...), custom_call_target="tpu_custom_call" | custom-call | tf_op jit(solution)/shard_map/pallas_call | solution.py:518
  40.4 1.1 %shard_map.137 = (f32[256,256]{1,0:T(8,128)}, f32[256,256]{1,0:T(8,128)}, f32[256,256]{1,0:T(8,128)}, f32[256,128]{1,0:T(8,128)}, f32[128,256]{1,0:T(8,128)}, /*index=5*/f32[256,256]{1,0:T(8,128)}) custom-call(f32[256,256]{1,0:T(8,128)S(1)} %get-tuple-element.12.refs_0_, f32[256,256]{1,0:T(8,128)S(1)} %get-tuple-element.13.refs_1_, ...), custom_call_target="tpu_custom_call" | custom-call | tf_op jit(solution)/shard_map/pallas_call | solution.py:581
